TPU v7x, 32 devices: a whole 2x2x4 slice. The times are simulated.
32 devices in a mesh: batch: 8 (over z, x), mp: 4 (over y, core).
Axes of the slice: x: 2, y: 2, z: 4, core: 2. Of those that a mesh axis runs over, the one named last changes fastest.
Arguments:
- image_states: bfloat16 [96, 197, 768], P('batch'), may hold values from -6 to 6
- text_states: bfloat16 [96, 40, 768], P('batch'), may hold values from -6 to 6
- caption_lengths: int32 [96], P('batch'), may hold values from 8 to 40, as said below
- image_cotangent: bfloat16 [96, 197, 768], P('batch'), may hold values from -6 to 6
- text_cotangent: bfloat16 [96, 40, 768], P('batch'), may hold values from -6 to 6
- first_gain: float32 [768], replicated, may hold values from 0.5 to 1.5
- first_shift: float32 [768], replicated, may hold values from -0.6 to 0.6
- query_key_value: bfloat16 [768, 3, 768], P(None, None, 'mp'), may hold values from -0.21875 to 0.21875
- query_value_bias: float32 [2, 768], P(None, 'mp'), may hold values from -1.2 to 1.2
- output_weight: bfloat16 [768, 768], P('mp'), may hold values from -1.25 to 1.25
- output_bias: float32 [768], replicated, may hold values from -0.6 to 0.6
- attention_scale: float32 [768], replicated, may hold values from 0.5 to 1.5
- expert_gain: float32 [2, 768], replicated, may hold values from 0.5 to 1.5
- expert_shift: float32 [2, 768], replicated, may hold values from -0.6 to 0.6
- expert_up: bfloat16 [2, 768, 3072], P(None, None, 'mp'), may hold values from -0.21875 to 0.21875
- expert_up_bias: float32 [2, 3072], P(None, 'mp'), may hold values from -1.2 to 1.2
- expert_down: bfloat16 [2, 3072, 768], P(None, 'mp'), may hold values from -0.109375 to 0.109375
- expert_down_bias: float32 [2, 768], replicated, may hold values from -0.6 to 0.6
- feedforward_scale: float32 [768], replicated, may hold values from 0.5 to 1.5
- head_gain: float32 [2, 768], replicated, may hold values from 0.5 to 1.5
- head_shift: float32 [2, 768], replicated, may hold values from -0.6 to 0.6
- head_weight: bfloat16 [2, 768, 768], replicated, may hold values from -0.21875 to 0.21875
- logit_scale: float32 [1], replicated, may hold values from 3.7 to 4.4
Outputs:
- image_output: bfloat16 [96, 197, 768], P('batch')
- text_output: bfloat16 [96, 40, 768], P('batch')
- contrast_loss: float32 [1], replicated
- image_grad: bfloat16 [96, 197, 768], P('batch')
- text_grad: bfloat16 [96, 40, 768], P('batch')
- grad_first_gain: float32 [768], P('batch')
- grad_first_shift: float32 [768], P('batch')
- grad_query_key_value: float32 [768, 3, 768], P('batch', None, 'mp')
- grad_query_value_bias: float32 [2, 768], P(None, 'mp')
- grad_output_weight: float32 [768, 768], P('mp', 'batch')
- grad_output_bias: float32 [768], P('batch')
- grad_attention_scale: float32 [768], P('batch')
- grad_expert_gain: float32 [2, 768], P(None, 'batch')
- grad_expert_shift: float32 [2, 768], P(None, 'batch')
- grad_expert_up: float32 [2, 768, 3072], P(None, 'batch', 'mp')
- grad_expert_up_bias: float32 [2, 3072], P(None, 'mp')
- grad_expert_down: float32 [2, 3072, 768], P(None, 'mp', 'batch')
- grad_expert_down_bias: float32 [2, 768], P(None, 'batch')
- grad_feedforward_scale: float32 [768], P('batch')
- grad_head_gain: float32 [2, 768], P(None, 'batch')
- grad_head_shift: float32 [2, 768], P(None, 'batch')
- grad_head_weight: float32 [2, 768, 768], P(None, 'batch')
- grad_logit_scale: float32 [1], replicated
Inputs may be any that keep to these rules, and one draw needn't show every extreme that they name: Caption p occupies positions 0 to caption_lengths[p] - 1 of its row; the rest is padding. In every draw some caption has all 40 positions.
All inputs are finite; a program needn't handle non-finite values.
Results may differ from a plain program's by a relative error of at most 0.02.
Values may be sent and summed in bfloat16 or wider, within the bound.
A program may use at most 256 MiB of HBM per device.

v0:
```python
import jax
import jax.numpy as jnp
from jax import lax
from jax.sharding import PartitionSpec as P

HEAD_DIM = 64


precise = lax.Precision.HIGHEST


def layer_norm(values, scales, shifts):
    centred = values - jnp.mean(values, axis=-1, keepdims=True)
    variance = jnp.mean(centred * centred, axis=-1, keepdims=True)
    return centred * lax.rsqrt(variance + 1e-05) * scales + shifts


def norm_backward(values, scales, shifts, upstream):
    result, pullback = jax.vjp(layer_norm, values, scales, shifts)
    return pullback(upstream)


def unit_rows(values):
    return values * lax.rsqrt(jnp.sum(values * values, axis=-1, keepdims=True) + 1e-06)


def exact_gelu(values):
    return jax.nn.gelu(values, approximate=False)


def product(left_side, right_side):
    return jnp.dot(left_side, right_side, preferred_element_type=jnp.float32)


def against(left_side, right_side):
    return lax.dot_general(
        left_side, right_side, (((1,), (1,)), ((), ())), preferred_element_type=jnp.float32
    )


def transposed(left_side, right_side):
    return lax.dot_general(
        left_side, right_side, (((0,), (0,)), ((), ())), preferred_element_type=jnp.float32
    )


def exact_dot(left_side, right_side):
    return jnp.dot(left_side, right_side, precision=precise, preferred_element_type=jnp.float32)


def by_modality(image_row, values):
    return jnp.stack(
        [
            jnp.sum(jnp.where(image_row, values, 0.0), axis=0),
            jnp.sum(jnp.where(image_row, 0.0, values), axis=0),
        ]
    )


def score_block(query_heads, key_heads, key_mask):
    raw_scores = jnp.einsum(
        "gqhe,gkhe->ghqk", query_heads, key_heads, preferred_element_type=jnp.float32
    ) * HEAD_DIM ** (-0.5)
    if key_mask is None:
        return raw_scores
    return jnp.where(key_mask[:, None, None, :], raw_scores, -1000000000.0)


def split_parts(projected, groups, positions):
    split_heads = projected.reshape(groups, positions, 3, -1, HEAD_DIM)
    return (split_heads[:, :, 0], split_heads[:, :, 1], split_heads[:, :, 2])


def attention_forward(projected, groups, positions, key_mask):
    query_heads, key_heads, value_heads = split_parts(projected, groups, positions)
    scores = score_block(query_heads, key_heads, key_mask)
    maximum = jnp.max(scores, axis=-1, keepdims=True)
    summed = jnp.sum(jnp.exp(scores - maximum), axis=-1, keepdims=True)
    log_total = maximum + jnp.log(summed)
    weights = jnp.exp(scores - log_total).astype(jnp.bfloat16)
    mixed_heads = jnp.einsum(
        "ghqk,gkhe->gqhe", weights, value_heads, preferred_element_type=jnp.float32
    )
    return (mixed_heads.astype(jnp.bfloat16).reshape(groups * positions, -1), log_total)


def attention_backward(projected, dmixed, log_total, groups, positions, key_mask):
    query_heads, key_heads, value_heads = split_parts(projected, groups, positions)
    scores = score_block(query_heads, key_heads, key_mask)
    weights = jnp.exp(scores - log_total)
    weights_low = weights.astype(jnp.bfloat16)
    upstream = dmixed.reshape(groups, positions, -1, HEAD_DIM)
    dvalues = jnp.einsum(
        "ghqk,gqhe->gkhe", weights_low, upstream, preferred_element_type=jnp.float32
    )
    dweights = jnp.einsum(
        "gqhe,gkhe->ghqk", upstream, value_heads, preferred_element_type=jnp.float32
    )
    dscores = weights * (dweights - jnp.sum(weights * dweights, axis=-1, keepdims=True))
    dscores = dscores.astype(jnp.bfloat16)
    dqueries = jnp.einsum(
        "ghqk,gkhe->gqhe", dscores, key_heads, preferred_element_type=jnp.float32
    ) * HEAD_DIM ** (-0.5)
    dkey_heads = jnp.einsum(
        "ghqk,gqhe->gkhe", dscores, query_heads, preferred_element_type=jnp.float32
    ) * HEAD_DIM ** (-0.5)
    stacked = jnp.stack([dqueries, dkey_heads, dvalues], axis=2).astype(jnp.bfloat16)
    return stacked.reshape(groups * positions, -1)


def per_device(
    image_states,
    text_states,
    caption_lengths,
    image_cotangent,
    text_cotangent,
    first_gain,
    first_shift,
    query_key_value,
    query_value_bias,
    output_weight,
    output_bias,
    attention_scale,
    expert_gain,
    expert_shift,
    expert_up,
    expert_up_bias,
    expert_down,
    expert_down_bias,
    feedforward_scale,
    head_gain,
    head_shift,
    head_weight,
    logit_scale,
):
    pair_count, patches, model_width = image_states.shape
    caption = text_states.shape[1]
    image_count = pair_count * patches
    text_count = pair_count * caption
    total_rows = image_count + text_count
    local_width = query_key_value.shape[2]
    states = jnp.concatenate(
        [
            image_states.reshape(image_count, model_width),
            text_states.reshape(text_count, model_width),
        ]
    ).astype(jnp.float32)
    key_mask = jnp.arange(caption, dtype=jnp.int32)[None, :] < caption_lengths[:, None]
    image_row = (jnp.arange(total_rows, dtype=jnp.int32) < image_count)[:, None]
    gain_rows = jnp.where(image_row, expert_gain[0], expert_gain[1])
    shift_rows = jnp.where(image_row, expert_shift[0], expert_shift[1])
    down_bias_rows = jnp.where(image_row, expert_down_bias[0], expert_down_bias[1])
    normed = layer_norm(states, first_gain, first_shift).astype(jnp.bfloat16)
    weight_flat = query_key_value.reshape(model_width, 3 * local_width)
    bias_full = jnp.concatenate(
        [query_value_bias[0], jnp.zeros_like(query_value_bias[0]), query_value_bias[1]]
    )
    projected = (product(normed, weight_flat) + bias_full).astype(jnp.bfloat16)
    image_mixed, image_total = attention_forward(projected[:image_count], pair_count, patches, None)
    text_mixed, text_total = attention_forward(
        projected[image_count:], pair_count, caption, key_mask
    )
    mixed_heads = jnp.concatenate([image_mixed, text_mixed])
    attention_part = product(mixed_heads, output_weight)
    attention_out = lax.psum(attention_part, "mp")
    attention_full = attention_out + output_bias
    attended = states + attention_scale * attention_full
    expert_low = layer_norm(attended, gain_rows, shift_rows).astype(jnp.bfloat16)
    expert_inputs = [expert_low[:image_count], expert_low[image_count:]]
    upwards = []
    activations = []
    partials = []
    for modality in range(2):
        upward = product(expert_inputs[modality], expert_up[modality]) + expert_up_bias[modality]
        activated = exact_gelu(upward).astype(jnp.bfloat16)
        upwards.append(upward)
        activations.append(activated)
        partials.append(product(activated, expert_down[modality]))
    expert_part = jnp.concatenate(partials)
    downward = lax.psum(expert_part, "mp")
    branch_full = downward + down_bias_rows
    final = attended + feedforward_scale * branch_full
    final_low = final.astype(jnp.bfloat16)
    class_rows = (
        final[:image_count].reshape(pair_count, patches, model_width)[:, 0],
        final[image_count:].reshape(pair_count, caption, model_width)[:, 0],
    )
    image_output = final_low[:image_count].reshape(pair_count, patches, model_width)
    text_output = final_low[image_count:].reshape(pair_count, caption, model_width)
    head_inputs = []
    projections = []
    embeddings = []
    for modality in range(2):
        head_in = layer_norm(
            class_rows[modality], head_gain[modality], head_shift[modality]
        ).astype(jnp.bfloat16)
        projection = product(head_in, head_weight[modality])
        head_inputs.append(head_in)
        projections.append(projection)
        embeddings.append(unit_rows(projection).astype(jnp.bfloat16))
    image_embed, text_embed = embeddings
    image_float = image_embed.astype(jnp.float32)
    text_float = text_embed.astype(jnp.float32)
    sharpness = jnp.exp(logit_scale[0])
    total_pairs = pair_count * lax.axis_size("batch")
    diagonal = sharpness * jnp.sum(image_float * text_float, axis=-1)
    lowest = jnp.full((pair_count,), -1e30, jnp.float32)
    row_max = lowest
    col_max = lowest
    row_logits = sharpness * against(
        image_embed, lax.all_gather(text_embed, "batch", axis=0, tiled=True)
    )
    col_logits = sharpness * against(
        text_embed, lax.all_gather(image_embed, "batch", axis=0, tiled=True)
    )
    row_new = jnp.maximum(row_max, jnp.max(row_logits, axis=1))
    row_sum = jnp.sum(jnp.exp(row_logits - row_new[:, None]), axis=1)
    col_new = jnp.maximum(col_max, jnp.max(col_logits, axis=1))
    col_sum = jnp.sum(jnp.exp(col_logits - col_new[:, None]), axis=1)
    row_max, row_sum, col_max, col_sum = (row_new, row_sum, col_new, col_sum)
    row_lse = row_max + jnp.log(row_sum)
    col_lse = col_max + jnp.log(col_sum)
    image_piece = lax.all_gather(image_float, "batch", axis=0, tiled=True)
    text_piece = lax.all_gather(text_float, "batch", axis=0, tiled=True)
    row_piece = lax.all_gather(row_lse, "batch", axis=0, tiled=True)
    col_piece = lax.all_gather(col_lse, "batch", axis=0, tiled=True)
    row_logits = sharpness * against(image_embed, text_piece.astype(jnp.bfloat16))
    row_own = jnp.exp(row_logits - row_lse[:, None])
    row_weights = row_own + jnp.exp(row_logits - col_piece[None, :])
    col_logits = sharpness * against(text_embed, image_piece.astype(jnp.bfloat16))
    col_own = jnp.exp(col_logits - col_lse[:, None])
    col_weights = col_own + jnp.exp(col_logits - row_piece[None, :])
    image_acc = exact_dot(row_weights, text_piece)
    text_acc = exact_dot(col_weights, image_piece)
    slope_sum = jnp.sum(row_own * row_logits) + jnp.sum(col_own * col_logits)
    loss_part = jnp.sum(row_lse - diagonal) + jnp.sum(col_lse - diagonal)
    slope_part = slope_sum - 2.0 * jnp.sum(diagonal)
    coefficient = sharpness / (2 * total_pairs)
    embed_grads = (
        coefficient * (image_acc - 2.0 * text_float),
        coefficient * (text_acc - 2.0 * image_float),
    )
    cotangents = (image_cotangent.astype(jnp.float32), text_cotangent.astype(jnp.float32))
    head_weight_grads = []
    head_gain_grads = []
    head_shift_grads = []
    dfinals = []
    for modality in range(2):
        unused, unit_pull = jax.vjp(unit_rows, projections[modality])
        dprojection = unit_pull(embed_grads[modality])[0].astype(jnp.bfloat16)
        head_weight_grads.append(transposed(head_inputs[modality], dprojection))
        dhead_in = against(dprojection, head_weight[modality])
        dclass, dgain, dshift = norm_backward(
            class_rows[modality], head_gain[modality], head_shift[modality], dhead_in
        )
        head_gain_grads.append(dgain)
        head_shift_grads.append(dshift)
        dfinals.append(cotangents[modality].at[:, 0].add(dclass).reshape(-1, model_width))
    dfinal_own = jnp.concatenate(dfinals)
    scale_grad = jnp.sum(dfinal_own * branch_full, axis=0)
    grad_expert_down_bias = by_modality(image_row, dfinal_own) * feedforward_scale
    down_grads = []
    up_bias_grads = []
    up_grads = []
    partial_back = []
    for modality in range(2):
        ddown = (feedforward_scale * dfinals[modality]).astype(jnp.bfloat16)
        down_grads.append(transposed(activations[modality], ddown))
        dactivated = against(ddown, expert_down[modality])
        unused, gelu_pull = jax.vjp(exact_gelu, upwards[modality])
        dupward = gelu_pull(dactivated)[0]
        up_bias_grads.append(jnp.sum(dupward, axis=0))
        dupward_low = dupward.astype(jnp.bfloat16)
        up_grads.append(transposed(expert_inputs[modality], dupward_low))
        partial_back.append(against(dupward_low, expert_up[modality]))
    back_part = jnp.concatenate(partial_back)
    dexpert_in = lax.psum(back_part.astype(jnp.bfloat16), "mp").astype(jnp.float32)
    dnorm_two, dgain_rows, dshift_rows = norm_backward(attended, gain_rows, shift_rows, dexpert_in)
    grad_expert_gain = by_modality(image_row, dgain_rows)
    grad_expert_shift = by_modality(image_row, dshift_rows)
    dattended = dfinal_own + dnorm_two
    grad_expert_up = jnp.stack(up_grads)
    grad_expert_down = jnp.stack(down_grads)
    grad_head_gain = jnp.stack(head_gain_grads)
    grad_head_shift = jnp.stack(head_shift_grads)
    grad_head_weight = jnp.stack(head_weight_grads)
    grad_attention_scale = jnp.sum(dattended * attention_full, axis=0)
    grad_output_bias = jnp.sum(dattended, axis=0) * attention_scale
    dattention = (attention_scale * dattended).astype(jnp.bfloat16)
    grad_output_weight = transposed(mixed_heads, dattention)
    dmixed = against(dattention, output_weight).astype(jnp.bfloat16)
    image_dprojected = attention_backward(
        projected[:image_count], dmixed[:image_count], image_total, pair_count, patches, None
    )
    text_dprojected = attention_backward(
        projected[image_count:], dmixed[image_count:], text_total, pair_count, caption, key_mask
    )
    dprojected = jnp.concatenate([image_dprojected, text_dprojected])
    column_sums = jnp.sum(dprojected.astype(jnp.float32), axis=0).reshape(3, local_width)
    grad_query_value_bias = jnp.stack([column_sums[0], column_sums[2]])
    grad_query_key_value = transposed(normed, dprojected).reshape(model_width, 3, local_width)
    normed_part = against(dprojected, weight_flat)
    dnormed = lax.psum(normed_part.astype(jnp.bfloat16), "mp").astype(jnp.float32)
    dnorm_one, grad_first_gain, grad_first_shift = norm_backward(
        states, first_gain, first_shift, dnormed
    )
    dstates = (dattended + dnorm_one).astype(jnp.bfloat16)
    (
        grad_first_gain,
        grad_first_shift,
        grad_query_key_value,
        grad_output_weight,
        grad_output_bias,
        grad_attention_scale,
        grad_expert_gain,
        grad_expert_shift,
        grad_expert_up,
        grad_expert_down,
        grad_expert_down_bias,
        scale_grad,
        grad_head_gain,
        grad_head_shift,
        grad_head_weight,
    ) = (
        lax.psum_scatter(grad_first_gain, "batch", scatter_dimension=0, tiled=True),
        lax.psum_scatter(grad_first_shift, "batch", scatter_dimension=0, tiled=True),
        lax.psum_scatter(grad_query_key_value, "batch", scatter_dimension=0, tiled=True),
        lax.psum_scatter(grad_output_weight, "batch", scatter_dimension=1, tiled=True),
        lax.psum_scatter(grad_output_bias, "batch", scatter_dimension=0, tiled=True),
        lax.psum_scatter(grad_attention_scale, "batch", scatter_dimension=0, tiled=True),
        lax.psum_scatter(grad_expert_gain, "batch", scatter_dimension=1, tiled=True),
        lax.psum_scatter(grad_expert_shift, "batch", scatter_dimension=1, tiled=True),
        lax.psum_scatter(grad_expert_up, "batch", scatter_dimension=1, tiled=True),
        lax.psum_scatter(grad_expert_down, "batch", scatter_dimension=2, tiled=True),
        lax.psum_scatter(grad_expert_down_bias, "batch", scatter_dimension=1, tiled=True),
        lax.psum_scatter(scale_grad, "batch", scatter_dimension=0, tiled=True),
        lax.psum_scatter(grad_head_gain, "batch", scatter_dimension=1, tiled=True),
        lax.psum_scatter(grad_head_shift, "batch", scatter_dimension=1, tiled=True),
        lax.psum_scatter(grad_head_weight, "batch", scatter_dimension=1, tiled=True),
    )
    loss_total, slope_total, grad_query_value_bias, grad_expert_up_bias = lax.psum(
        (loss_part, slope_part, grad_query_value_bias, jnp.stack(up_bias_grads)), "batch"
    )
    contrast_loss = (loss_total / (2 * total_pairs)).reshape(1)
    grad_logit_scale = (slope_total / (2 * total_pairs)).reshape(1)
    image_grad = dstates[:image_count].reshape(pair_count, patches, model_width)
    text_grad = dstates[image_count:].reshape(pair_count, caption, model_width)
    return (
        image_output,
        text_output,
        contrast_loss,
        image_grad,
        text_grad,
        grad_first_gain,
        grad_first_shift,
        grad_query_key_value,
        grad_query_value_bias,
        grad_output_weight,
        grad_output_bias,
        grad_attention_scale,
        grad_expert_gain,
        grad_expert_shift,
        grad_expert_up,
        grad_expert_up_bias,
        grad_expert_down,
        grad_expert_down_bias,
        scale_grad,
        grad_head_gain,
        grad_head_shift,
        grad_head_weight,
        grad_logit_scale,
    )


def solution(mesh):
    return jax.shard_map(
        per_device,
        mesh=mesh,
        in_specs=(
            P("batch", None, None),
            P("batch", None, None),
            P("batch"),
            P("batch", None, None),
            P("batch", None, None),
            P(),
            P(),
            P(None, None, "mp"),
            P(None, "mp"),
            P("mp", None),
            P(),
            P(),
            P(),
            P(),
            P(None, None, "mp"),
            P(None, "mp"),
            P(None, "mp", None),
            P(),
            P(),
            P(),
            P(),
            P(),
            P(),
        ),
        out_specs=(
            P("batch", None, None),
            P("batch", None, None),
            P(),
            P("batch", None, None),
            P("batch", None, None),
            P("batch"),
            P("batch"),
            P("batch", None, "mp"),
            P(None, "mp"),
            P("mp", "batch"),
            P("batch"),
            P("batch"),
            P(None, "batch"),
            P(None, "batch"),
            P(None, "batch", "mp"),
            P(None, "mp"),
            P(None, "mp", "batch"),
            P(None, "batch"),
            P("batch"),
            P(None, "batch"),
            P(None, "batch"),
            P(None, "batch", None),
            P(),
        ),
        check_vma=False,
    )
```

profile of v0, /device:TPU:0, one launch (start us, length us, event | category | flops | bytes accessed | tf_op | source)
XLA Modules:
  0.0 1679.4 jit_solution(10901012707866268982)
XLA Ops:
  43.8 13.1 reshape.458
  76.2 161.1 %all-reduce.16.cloned.1.call-done = f32[2844,768]{1,0:T(8,128)} async-done(((f32[2844,768]{1,0:T(8,128)}), f32[2844,768]{1,0:T(8,128)}) %all-reduce.16.cloned.1.call-update) | async-done | bytes 8736784 | tf_op jit(solution)/shard_map/psum | solution.py:165
  256.1 19.7 %multiply_convert_fusion.4 = (bf16[2364,768]{1,0:T(8,128)(2,1)S(1)}, f32[2364,768]{1,0:T(8,128)}, f32[2364,768]{1,0:T(8,128)}) fusion(f32[768]{0:T(1024)S(1)} %get-tuple-element.188, bf16[2,768,768]{2,1,0:T(8,128)(2,1)S(1)} %copy-done.114, bf16[2844,768]{1,0:T(8,128)(2,1)S(1)} %fusion.12), kind=kOutput, calls=%fused_computation.54 | convolution fusion | flops 2908514304 | bytes 22976512 | tf_op jit(solution)/shard_map/dot_general | solution.py:32
  298.4 150.6 %all-reduce.18.cloned.1.call-done = f32[2844,768]{1,0:T(8,128)} async-done(((f32[2844,768]{1,0:T(8,128)}), f32[2844,768]{1,0:T(8,128)}) %all-reduce.18.cloned.1.call-update) | async-done | bytes 8736784 | tf_op jit(solution)/shard_map/psum | solution.py:180
  449.0 9.2 fusion.195
  462.8 8.6 reshape.464
  476.6 30.7 %all-gather.1 = bf16[8,12,768]{2,1,0:T(8,128)(2,1)S(1)} all-gather(bf16[1,12,768]{2,1,0:T(8,128)(2,1)S(1)} %bitcast.295), channel_id=1, replica_groups=mesh['batch'=8,'mp'=4] {'batch'}, dimensions={0}, use_global_device_ids=true | all-gather | bytes 165888 | tf_op jit(solution)/shard_map/all_gather | solution.py:214
  507.8 30.6 %all-gather = bf16[8,12,768]{2,1,0:T(8,128)(2,1)S(1)} all-gather(bf16[1,12,768]{2,1,0:T(8,128)(2,1)S(1)} %bitcast.296), channel_id=1, replica_groups=mesh['batch'=8,'mp'=4] {'batch'}, dimensions={0}, use_global_device_ids=true | all-gather | bytes 165888 | tf_op jit(solution)/shard_map/all_gather | solution.py:211
  538.7 31.0 %all-gather.3 = f32[8,12,768]{2,1,0:T(8,128)S(1)} all-gather(f32[1,12,768]{2,1,0:T(8,128)S(1)} %get-tuple-element.226), channel_id=1, replica_groups=mesh['batch'=8,'mp'=4] {'batch'}, dimensions={0}, use_global_device_ids=true | all-gather | bytes 331776 | tf_op jit(solution)/shard_map/all_gather | solution.py:223
  571.1 21.4 %all-reduce.9 = (f32[96]{0:T(128)S(1)}, f32[96]{0:T(128)S(1)}) all-reduce(f32[96]{0:T(128)S(1)} %get-tuple-element.224, f32[96]{0:T(128)S(1)} %get-tuple-element.222), channel_id=1, replica_groups=mesh['batch'=8,'mp'=4] {'batch'}, use_global_device_ids=true, to_apply=%add.1 | all-reduce | flops 192 | bytes 1536
  595.1 31.0 %all-gather.2 = f32[8,12,768]{2,1,0:T(8,128)S(1)} all-gather(f32[1,12,768]{2,1,0:T(8,128)S(1)} %get-tuple-element.218), channel_id=1, replica_groups=mesh['batch'=8,'mp'=4] {'batch'}, dimensions={0}, use_global_device_ids=true | all-gather | bytes 331776 | tf_op jit(solution)/shard_map/all_gather | solution.py:224
  646.0 10.9 fusion.208
  663.9 9.4 reshape.468
  674.3 73.7 %all-reduce.20.cloned.1.call-done = bf16[2844,768]{1,0:T(8,128)(2,1)} async-done(((bf16[2844,768]{1,0:T(8,128)(2,1)}), bf16[2844,768]{1,0:T(8,128)(2,1)}) %all-reduce.20.cloned.1.call-update) | async-done | bytes 4368400 | tf_op jit(solution)/shard_map/psum | solution.py:277
  748.0 15.6 multiply_reduce_fusion
  763.7 11.8 fusion.190
  775.5 10.8 multiply_reduce_fusion.1
  814.4 9.9 multiply_reduce_fusion.3
  864.7 8.5 convert_element_type.184
  873.2 7.5 convolution_convert_fusion.1
  892.0 8.2 copy.193
  901.3 7.5 fusion.97
  949.0 56.9 %reduce-scatter.32.cloned.1.call-done = f32[96,2]{1,0:T(8,128)} async-done(((f32[768,2]{1,0:T(8,128)}), f32[96,2]{1,0:T(8,128)}) %reduce-scatter.32.cloned.1.call-update) | async-done | bytes 784
  1007.4 62.6 %reduce-scatter.34.cloned.1.call-done = f32[96,2]{1,0:T(8,128)} async-done(((f32[768,2]{1,0:T(8,128)}), f32[96,2]{1,0:T(8,128)}) %reduce-scatter.34.cloned.1.call-update) | async-done | bytes 784
  1071.4 63.7 %reduce-scatter.28.cloned.1.call-done = f32[96,192]{1,0:T(8,128)} async-done(((f32[768,192]{1,0:T(8,128)}), f32[96,192]{1,0:T(8,128)}) %reduce-scatter.28.cloned.1.call-update) | async-done | bytes 73744
  1136.8 88.3 %all-reduce.22.cloned.1.call-done = bf16[2844,768]{1,0:T(8,128)(2,1)} async-done(((bf16[2844,768]{1,0:T(8,128)(2,1)}), bf16[2844,768]{1,0:T(8,128)(2,1)}) %all-reduce.22.cloned.1.call-update) | async-done | bytes 4368400 | tf_op jit(solution)/shard_map/psum | solution.py:303
  1236.7 39.9 %all-reduce.8 = (f32[]{:T(128)}, f32[768]{0:T(1024)S(1)}, f32[768]{0:T(1024)S(1)}, f32[2,192]{1,0:T(2,128)}, f32[768]{0:T(1024)S(1)}, /*index=5*/f32[768]{0:T(10...) all-reduce(f32[]{:T(128)S(6)} %add.286, ...), channel_id=1, replica_groups=mesh['batch'=8,'mp'=4] {'batch'}, use_global_device_ids=true, to_apply=%region_23.24 | all-reduce | flops 5762 | bytes 46096 | tf_op jit(solution)/shard_map/psum | solution.py:341
  1276.6 8.9 add_convert_fusion
  1297.0 102.3 %all-reduce.24.cloned.1.call-done = f32[2,768,768]{1,0,2:T(2,128)} async-done(((f32[2,768,768]{1,0,2:T(2,128)}), f32[2,768,768]{1,0,2:T(2,128)}) %all-reduce.24.cloned.1.call-update) | async-done | bytes 4718608
  1401.4 70.2 %reduce-scatter.22.cloned.1.call-done = f32[96,3,192]{2,0,1:T(8,128)} async-done(((f32[768,3,192]{2,0,1:T(8,128)}), f32[96,3,192]{2,0,1:T(8,128)}) %reduce-scatter.22.cloned.1.call-update) | async-done | bytes 221200 | tf_op jit(solution)/shard_map/reduce_scatter | solution.py:327
  1471.6 99.0 %reduce-scatter.24.cloned.1.call-done = f32[2,96,768]{2,1,0:T(8,128)} async-done(((f32[2,768,768]{2,1,0:T(8,128)}), f32[2,96,768]{2,1,0:T(8,128)}) %reduce-scatter.24.cloned.1.call-update) | async-done | bytes 589840 | tf_op jit(solution)/shard_map/reduce_scatter | solution.py:333
  1570.6 99.6 %reduce-scatter.26.cloned.1.call-done = f32[2,96,768]{2,1,0:T(8,128)} async-done(((f32[2,768,768]{2,1,0:T(8,128)}), f32[2,96,768]{2,1,0:T(8,128)}) %reduce-scatter.26.cloned.1.call-update) | async-done | bytes 589840 | tf_op jit(solution)/shard_map/reduce_scatter | solution.py:339
  (479 shorter events, 282.3 us)
Async XLA Ops:
  7.2 230.1 %all-reduce.16.cloned.1.call-start = ((), (), s32[]{:S(2)}) async-start(), calls=%async_computation.9 | async-start | bytes 17498112 | tf_op jit(solution)/shard_map/psum | solution.py:165
  75.4 161.9 %copy-start.63 = (f32[768]{0:T(1024)S(1)}, f32[768]{0:T(1024)}, u32[]{:S(2)}) copy-start(f32[768]{0:T(1024)} %param.38) | copy-start | bytes 9220
  75.4 161.9 %copy-start.76 = (f32[768]{0:T(1024)S(1)}, f32[768]{0:T(1024)}, u32[]{:S(2)}) copy-start(f32[768]{0:T(1024)} %param.37) | copy-start | bytes 9220
  75.4 373.6 %all-reduce.18.cloned.1.call-start = ((), (), s32[]{:S(2)}) async-start(), calls=%async_computation.10 | async-start | bytes 17498112 | tf_op jit(solution)/shard_map/psum | solution.py:180
  76.2 168.3 %copy-start.70 = (f32[768]{0:T(1024)}, f32[768]{0:T(1024)S(1)}, u32[]{:S(2)}) copy-start(f32[768]{0:T(1024)S(1)} %get-tuple-element.190) | copy-start | bytes 9220
  76.2 168.3 %copy-start.72 = (f32[768]{0:T(1024)}, f32[768]{0:T(1024)S(1)}, u32[]{:S(2)}) copy-start(f32[768]{0:T(1024)S(1)} %get-tuple-element.191) | copy-start | bytes 9220
  289.9 458.1 %all-reduce.20.cloned.1.call-start = ((), (), s32[]{:S(2)}) async-start(), calls=%async_computation.11 | async-start | bytes 8749056 | tf_op jit(solution)/shard_map/psum | solution.py:277
  291.1 157.9 %copy-start.56 = (f32[768]{0:T(1024)S(1)}, f32[768]{0:T(1024)}, u32[]{:S(2)}) copy-start(f32[768]{0:T(1024)} %param.45) | copy-start | bytes 9220
  298.4 174.5 %copy-start.80 = (f32[768]{0:T(1024)}, f32[768]{0:T(1024)S(1)}, u32[]{:S(2)}) copy-start(f32[768]{0:T(1024)S(1)} %get-tuple-element.184) | copy-start | bytes 9220
  298.4 176.4 %copy-start.78 = (f32[768]{0:T(1024)}, f32[768]{0:T(1024)S(1)}, u32[]{:S(2)}) copy-start(f32[768]{0:T(1024)S(1)} %get-tuple-element.185) | copy-start | bytes 9220
  472.6 153.4 %copy-start.46 = (f32[12,1,768]{2,1,0:T(1,128)}, f32[12,1,768]{2,1,0:T(1,128)S(1)}, u32[]{:S(2)}) copy-start(f32[12,1,768]{2,1,0:T(1,128)S(1)} %get-tuple-element.245) | copy-start | bytes 110596
  472.6 156.6 %copy-start.44 = (f32[12,1,768]{2,1,0:T(1,128)}, f32[12,1,768]{2,1,0:T(1,128)S(1)}, u32[]{:S(2)}) copy-start(f32[12,1,768]{2,1,0:T(1,128)S(1)} %get-tuple-element.284) | copy-start | bytes 110596
  472.7 153.4 %copy-start.101 = (f32[12]{0:T(128)}, f32[12]{0:T(128)S(1)}, u32[]{:S(2)}) copy-start(f32[12]{0:T(128)S(1)} %broadcast_multiply_fusion.3) | copy-start | bytes 148
  472.9 153.2 %copy-start.107 = (f32[12]{0:T(128)}, f32[12]{0:T(128)S(1)}, u32[]{:S(2)}) copy-start(f32[12]{0:T(128)S(1)} %fusion.180) | copy-start | bytes 148
  474.6 154.7 %copy-start.103 = (f32[12]{0:T(128)}, f32[12]{0:T(128)S(1)}, u32[]{:S(2)}) copy-start(f32[12]{0:T(128)S(1)} %broadcast_multiply_fusion.4) | copy-start | bytes 148
  474.8 154.5 %copy-start.109 = (f32[12]{0:T(128)}, f32[12]{0:T(128)S(1)}, u32[]{:S(2)}) copy-start(f32[12]{0:T(128)S(1)} %fusion.179) | copy-start | bytes 148
  476.6 152.9 %copy-start.38 = (bf16[12,768]{1,0:T(8,128)(2,1)}, bf16[12,768]{1,0:T(8,128)(2,1)S(1)}, u32[]{:S(2)}) copy-start(bf16[12,768]{1,0:T(8,128)(2,1)S(1)} %get-tuple-element.227) | copy-start | bytes 55300
  507.5 126.9 %copy-start.40 = (bf16[12,768]{1,0:T(8,128)(2,1)}, bf16[12,768]{1,0:T(8,128)(2,1)S(1)}, u32[]{:S(2)}) copy-start(bf16[12,768]{1,0:T(8,128)(2,1)S(1)} %get-tuple-element.219) | copy-start | bytes 55300
  662.8 279.2 %reduce-scatter.36.cloned.1.call-start = ((), (), s32[]{:S(2)}) async-start(), calls=%async_computation.20 | async-start | bytes 442368
  663.8 279.6 %reduce-scatter.38.cloned.1.call-start = ((), (), s32[]{:S(2)}) async-start(), calls=%async_computation.21 | async-start | bytes 442368
  663.9 84.1 %copy-start.51 = (f32[2844]{0:T(1024)S(1)}, f32[2844]{0:T(1024)}, u32[]{:S(2)}) copy-start(f32[2844]{0:T(1024)} %copy-done.50) | copy-start | bytes 34132
  663.9 84.1 %copy-start.55 = (f32[2844]{0:T(1024)S(1)}, f32[2844]{0:T(1024)}, u32[]{:S(2)}) copy-start(f32[2844]{0:T(1024)} %copy-done.54) | copy-start | bytes 34132
  674.3 273.3 %reduce-scatter.30.cloned.1.call-start = ((), (), s32[]{:S(2)}) async-start(), calls=%async_computation.17 | async-start | bytes 442368
  840.2 165.8 %reduce-scatter.32.cloned.1.call-start = ((), (), s32[]{:S(2)}) async-start(), calls=%async_computation.18 | async-start | bytes 442368
  841.2 228.7 %reduce-scatter.34.cloned.1.call-start = ((), (), s32[]{:S(2)}) async-start(), calls=%async_computation.19 | async-start | bytes 442368
  844.4 290.7 %reduce-scatter.28.cloned.1.call-start = ((), (), s32[]{:S(2)}) async-start(), calls=%async_computation.16 | async-start | bytes 884736
  846.7 378.4 %all-reduce.22.cloned.1.call-start = ((), (), s32[]{:S(2)}) async-start(), calls=%async_computation.12 | async-start | bytes 8749056 | tf_op jit(solution)/shard_map/psum | solution.py:303
  880.7 518.6 %all-reduce.24.cloned.1.call-start = ((), (), s32[]{:S(2)}) async-start(), calls=%async_computation.22 | async-start | bytes 9437184
  900.3 571.3 %reduce-scatter.22.cloned.1.call-start = ((), (), s32[]{:S(2)}) async-start(), calls=%async_computation.13 | async-start | bytes 2654208 | tf_op jit(solution)/shard_map/reduce_scatter | solution.py:327
  911.9 658.8 %reduce-scatter.24.cloned.1.call-start = ((), (), s32[]{:S(2)}) async-start(), calls=%async_computation.14 | async-start | bytes 5308416 | tf_op jit(solution)/shard_map/reduce_scatter | solution.py:333
  922.3 747.9 %reduce-scatter.26.cloned.1.call-start = ((), (), s32[]{:S(2)}) async-start(), calls=%async_computation.15 | async-start | bytes 5308416 | tf_op jit(solution)/shard_map/reduce_scatter | solution.py:339
  1136.8 94.6 %copy-start.62 = (f32[2844]{0:T(1024)S(1)}, f32[2844]{0:T(1024)}, u32[]{:S(2)}) copy-start(f32[2844]{0:T(1024)} %copy-done.61) | copy-start | bytes 34132
  (109 other events, 919.6 us)
Sparse Core Ops, SparseCore 0:
  75.6 161.7 all-reduce.15
  290.0 159.0 all-reduce.17
  662.9 85.0 all-reduce.19
  751.4 61.4 reduce-scatter.35
  816.4 60.3 reduce-scatter.37
  880.9 60.3 reduce-scatter.29
  945.5 60.3 reduce-scatter.31
  1009.6 60.3 reduce-scatter.33
  1073.6 61.4 reduce-scatter.27
  1137.4 87.6 all-reduce.21
  1229.1 170.2 all-reduce.23
  1403.7 67.8 reduce-scatter.21
  1476.3 94.3 reduce-scatter.23
  1575.1 94.9 reduce-scatter.25
where the time goes:
time: 1690 us; the launch traced here: 1680 us
  waiting for transfers between devices  1030 us (61%)
  blocking collectives  185 us (11%)
  local copies, waits for them, and re-layouts  166 us (10%)
  matrix products  146 us (9%)
  other arithmetic  129 us (8%)
  between operations  25 us (1%)
    unnamed x21, waiting for transfers between devices  286 us
    psum x1, waiting for transfers between devices, per_device(): attention_out = lax.psum(attention_part, 'mp')  161 us
    psum x1, waiting for transfers between devices, per_device(): downward = lax.psum(expert_part, 'mp')  151 us
    reduce_scatter x1, waiting for transfers between devices, per_device(): lax.psum_scatter(grad_head_weight, 'batch', scatter_dimension=1, tiled=True)  99.6 us
    reduce_scatter x1, waiting for transfers between devices, per_device(): lax.psum_scatter(grad_expert_up, 'batch', scatter_dimension=1, tiled=True)  99 us
    psum x1, waiting for transfers between devices, per_device(): lax.psum(normed_part.astype(jnp.bfloat16), 'mp').astype(jnp.float32)  88.3 us
    psum x1, waiting for transfers between devices, per_device(): lax.psum(back_part.astype(jnp.bfloat16), 'mp').astype(jnp.float32)  73.7 us
    reduce_scatter x1, waiting for transfers between devices, per_device(): lax.psum_scatter(grad_query_key_value, 'batch', scatter_dimension=0, tile...  70.2 us
  transfers between devices with their start and end apart: 14, of which 11 were waited for; matrix products, arithmetic and copies ran while one was open for 15% of the time, Pallas kernels for 0%

commit v1 on v0

v1 whole, which is shorter than its diff:
```python
import functools

import jax
import jax.numpy as jnp
from jax import lax
from jax.experimental import pallas as pl
from jax.experimental.pallas import tpu as pltpu
from jax.sharding import PartitionSpec as P

HEAD_DIM = 64
F32 = jnp.float32
BF16 = jnp.bfloat16
NEG = -1e9
EPS = 1e-5
ORDER = (0, 2, 1, 3)

VMEM_LIMIT = 60 * 1024 * 1024


def params(**kw):
    return pltpu.CompilerParams(vmem_limit_bytes=VMEM_LIMIT, **kw)


def up16(n):
    return -(-n // 16) * 16


def dot(a, b):
    return jnp.dot(a, b, preferred_element_type=F32)


def dot_t(a, b):
    return lax.dot_general(a, b, (((1,), (1,)), ((), ())), preferred_element_type=F32)


def t_dot(a, b):
    return lax.dot_general(a, b, (((0,), (0,)), ((), ())), preferred_element_type=F32)


def normalise(x):
    c = x - jnp.mean(x, axis=-1, keepdims=True)
    v = jnp.mean(c * c, axis=-1, keepdims=True)
    r = lax.rsqrt(v + EPS)
    return c * r, r


def norm_back(n, r, dn):
    a = jnp.mean(dn, axis=-1, keepdims=True)
    b = jnp.mean(dn * n, axis=-1, keepdims=True)
    return (dn - a - n * b) * r


def gelu_parts(u):
    big = 0.5 * (1.0 + lax.erf(u * 0.7071067811865476))
    small = 0.3989422804014327 * jnp.exp(-0.5 * u * u)
    return big, small


def gelu_low(u):
    return (u * (0.5 * (1.0 + lax.erf(u * 0.7071067811865476)))).astype(BF16)


def softmax_rows(scores):
    m = jnp.max(scores, axis=-1, keepdims=True)
    e = jnp.exp(scores - m)
    return e * (1.0 / jnp.sum(e, axis=-1, keepdims=True))


def attend_kernel(dims, order, lens, img, txt, gain, shift, wt, bias, ow,
                  normed, qkv, mixed, keep, send, rows):
    patches, caption, ip, tp, quarter, width = dims
    i = pl.program_id(0)
    slab = ip + tp

    @pl.when(i == 0)
    def _():
        rows[...] = jnp.zeros_like(rows)

    def one_norm(p, c):
        rows[0:patches, :] = img[p].astype(F32)
        rows[ip:ip + caption, :] = txt[p].astype(F32)
        n, _ = normalise(rows[...])
        normed[p] = (n * gain[...] + shift[...]).astype(BF16)
        return c

    lax.fori_loop(0, quarter, one_norm, 0)
    model = normed.shape[-1]
    proj = dot_t(normed[...].reshape(quarter * slab, model), wt[...]) + bias[...]
    qkv[...] = proj.astype(BF16).reshape(quarter, slab, 3 * width)
    low = lax.broadcasted_iota(jnp.int32, (1, 128), 1) < HEAD_DIM
    img_ok = lax.broadcasted_iota(jnp.int32, (1, ip), 1) < patches
    txt_at = lax.broadcasted_iota(jnp.int32, (1, tp), 1)

    def one_pair(p, c):
        length = lens[order[i] * quarter + p]
        for lo, hi, ok in ((0, ip, img_ok), (ip, slab, txt_at < length)):
            for g in range(width // 128):
                q = qkv[p, lo:hi, g * 128:(g + 1) * 128] * jnp.asarray(HEAD_DIM ** -0.5, BF16)
                k = qkv[p, lo:hi, width + g * 128:width + (g + 1) * 128]
                v = qkv[p, lo:hi, 2 * width + g * 128:2 * width + (g + 1) * 128]
                outs = []
                for sel in (low, ~low):
                    s = dot_t(jnp.where(sel, q, jnp.zeros_like(q)), k)
                    w = softmax_rows(jnp.where(ok, s, NEG)).astype(BF16)
                    outs.append(dot(w, v))
                mixed[p, lo:hi, g * 128:(g + 1) * 128] = jnp.where(low, outs[0], outs[1]).astype(BF16)
        return c

    lax.fori_loop(0, quarter, one_pair, 0)
    part = dot(mixed[...].reshape(quarter * slab, width), ow[...])
    part = part.astype(BF16).reshape(quarter, slab, model)

    @pl.when(i < 2)
    def _():
        keep[...] = part

    @pl.when(i >= 2)
    def _():
        send[...] = part


def attend(dims, order, lens, img, txt, gain, shift, wt, bias, ow):
    patches, caption, ip, tp, quarter, width = dims
    model = img.shape[-1]
    slab = ip + tp
    pairs = 4 * quarter
    whole = lambda a: pl.BlockSpec(a.shape, lambda i, o, n: (0,) * a.ndim)
    block = lambda cols, at: pl.BlockSpec((quarter, slab, cols), at)
    return pl.pallas_call(
        functools.partial(attend_kernel, dims),
        grid_spec=pltpu.PrefetchScalarGridSpec(
            num_scalar_prefetch=2,
            grid=(4,),
            in_specs=[
                pl.BlockSpec((quarter, patches, model), lambda i, o, n: (o[i], 0, 0)),
                pl.BlockSpec((quarter, caption, model), lambda i, o, n: (o[i], 0, 0)),
                whole(gain), whole(shift), whole(wt), whole(bias), whole(ow),
            ],
            out_specs=[
                block(model, lambda i, o, n: (i, 0, 0)),
                block(3 * width, lambda i, o, n: (i, 0, 0)),
                block(width, lambda i, o, n: (i, 0, 0)),
                block(model, lambda i, o, n: (jnp.minimum(i, 1), 0, 0)),
                block(model, lambda i, o, n: (jnp.maximum(i - 2, 0), 0, 0)),
            ],
            scratch_shapes=[pltpu.VMEM((slab, model), F32)],
        ),
        out_shape=[
            jax.ShapeDtypeStruct((pairs, slab, model), BF16),
            jax.ShapeDtypeStruct((pairs, slab, 3 * width), BF16),
            jax.ShapeDtypeStruct((pairs, slab, width), BF16),
            jax.ShapeDtypeStruct((2 * quarter, slab, model), BF16),
            jax.ShapeDtypeStruct((2 * quarter, slab, model), BF16),
        ],
        compiler_params=params(),
        cost_estimate=pl.CostEstimate(
            flops=2 * pairs * slab * model * width * 4, bytes_accessed=30_000_000, transcendentals=0),
        name="attend",
    )(order, lens, img, txt, gain, shift, wt, bias, ow)


def residual_kernel(dims, order, keep, recv, img, txt, scale, bias, gain, shift, attended, expert, rows):
    patches, caption, ip, tp, quarter, width = dims

    @pl.when(pl.program_id(0) == 0)
    def _():
        rows[...] = jnp.zeros_like(rows)

    def one(p, c):
        rows[0:patches, :] = img[p].astype(F32)
        rows[ip:ip + caption, :] = txt[p].astype(F32)
        a = keep[p].astype(F32) + recv[p].astype(F32)
        x = rows[...] + scale[...] * (a + bias[...])
        attended[p] = x
        n, _ = normalise(x)
        expert[p, 0:ip, :] = (n[0:ip] * gain[0:1] + shift[0:1]).astype(BF16)
        expert[p, ip:, :] = (n[ip:] * gain[1:2] + shift[1:2]).astype(BF16)
        return c

    lax.fori_loop(0, quarter, one, 0)


def residual(dims, order, keep, recv, img, txt, scale, bias, gain, shift):
    patches, caption, ip, tp, quarter, width = dims
    model = img.shape[-1]
    slab = ip + tp
    whole = lambda a: pl.BlockSpec(a.shape, lambda i, o: (0,) * a.ndim)
    block = pl.BlockSpec((quarter, slab, model), lambda i, o: (i, 0, 0))
    return pl.pallas_call(
        functools.partial(residual_kernel, dims),
        grid_spec=pltpu.PrefetchScalarGridSpec(
            num_scalar_prefetch=1,
            grid=(2,),
            in_specs=[
                block, block,
                pl.BlockSpec((quarter, patches, model), lambda i, o: (o[i], 0, 0)),
                pl.BlockSpec((quarter, caption, model), lambda i, o: (o[i], 0, 0)),
                whole(scale), whole(bias), whole(gain), whole(shift),
            ],
            out_specs=[block, block],
            scratch_shapes=[pltpu.VMEM((slab, model), F32)],
        ),
        out_shape=[
            jax.ShapeDtypeStruct((2 * quarter, slab, model), F32),
            jax.ShapeDtypeStruct((2 * quarter, slab, model), BF16),
        ],
        compiler_params=params(),
        cost_estimate=pl.CostEstimate(flops=40_000_000, bytes_accessed=20_000_000, transcendentals=0),
        name="residual",
    )(order, keep, recv, img, txt, scale, bias, gain, shift)


def expert_kernel(dims, order, own, peer, img, txt, scale, up, up_bias, down,
                  act, dup, ddown, down_keep, down_send, dexp_keep, dexp_send, bias_grad, ins, rows):
    patches, caption, ip, tp, quarter, width = dims
    slab = ip + tp
    i = pl.program_id(0)
    model = own.shape[-1]

    @pl.when(i == 0)
    def _():
        rows[...] = jnp.zeros_like(rows)
        bias_grad[...] = jnp.zeros_like(bias_grad)

    @pl.when(i < 2)
    def _():
        ins[...] = own[...]

    @pl.when(i >= 2)
    def _():
        ins[...] = peer[...]

    at = lax.broadcasted_iota(jnp.int32, (slab, 1), 0)
    inner = (at != 0) & (at != ip)

    def one(p, c):
        rows[0:patches, :] = img[p].astype(F32)
        rows[ip:ip + caption, :] = txt[p].astype(F32)
        ddown[p] = jnp.where(inner, rows[...] * scale[...], 0.0).astype(BF16)
        return c

    lax.fori_loop(0, quarter, one, 0)
    for m, lo, hi in ((0, 0, ip), (1, ip, slab)):
        count = quarter * (hi - lo)
        e = ins[:, lo:hi, :].reshape(count, model)
        u = dot(e, up[m]) + up_bias[m:m + 1]
        big, small = gelu_parts(u)
        a = (u * big).astype(BF16)
        act[:, lo:hi, :] = a.reshape(quarter, hi - lo, -1)
        slope = big + u * small
        d = dot(a, down[m]).astype(BF16).reshape(quarter, hi - lo, model)
        g = ddown[:, lo:hi, :].reshape(count, model)
        du = dot_t(g, down[m]) * slope
        bias_grad[m:m + 1, :] += jnp.sum(du, axis=0, keepdims=True)
        low = du.astype(BF16)
        dup[:, lo:hi, :] = low.reshape(quarter, hi - lo, -1)
        x = dot_t(low, up[m]).astype(BF16).reshape(quarter, hi - lo, model)

        @pl.when(i < 2)
        def _():
            down_keep[:, lo:hi, :] = d
            dexp_keep[:, lo:hi, :] = x

        @pl.when(i >= 2)
        def _():
            down_send[:, lo:hi, :] = d
            dexp_send[:, lo:hi, :] = x


def experts(dims, order, own, peer, img, txt, scale, up, up_bias, down):
    patches, caption, ip, tp, quarter, width = dims
    model = own.shape[-1]
    hidden = up.shape[-1]
    slab = ip + tp
    pairs = 4 * quarter
    whole = lambda a: pl.BlockSpec(a.shape, lambda i, o: (0,) * a.ndim)
    first = pl.BlockSpec((quarter, slab, model), lambda i, o: (jnp.minimum(i, 1), 0, 0))
    last = pl.BlockSpec((quarter, slab, model), lambda i, o: (jnp.maximum(i - 2, 0), 0, 0))
    half = jax.ShapeDtypeStruct((2 * quarter, slab, model), BF16)
    return pl.pallas_call(
        functools.partial(expert_kernel, dims),
        grid_spec=pltpu.PrefetchScalarGridSpec(
            num_scalar_prefetch=1,
            grid=(4,),
            in_specs=[
                first, last,
                pl.BlockSpec((quarter, patches, model), lambda i, o: (o[i], 0, 0)),
                pl.BlockSpec((quarter, caption, model), lambda i, o: (o[i], 0, 0)),
                whole(scale), whole(up), whole(up_bias), whole(down),
            ],
            out_specs=[
                pl.BlockSpec((quarter, slab, hidden), lambda i, o: (i, 0, 0)),
                pl.BlockSpec((quarter, slab, hidden), lambda i, o: (i, 0, 0)),
                pl.BlockSpec((quarter, slab, model), lambda i, o: (i, 0, 0)),
                first, last, first, last,
                pl.BlockSpec((2, hidden), lambda i, o: (0, 0)),
            ],
            scratch_shapes=[pltpu.VMEM((quarter, slab, model), BF16), pltpu.VMEM((slab, model), F32)],
        ),
        out_shape=[
            jax.ShapeDtypeStruct((pairs, slab, hidden), BF16),
            jax.ShapeDtypeStruct((pairs, slab, hidden), BF16),
            jax.ShapeDtypeStruct((pairs, slab, model), BF16),
            half, half, half, half,
            jax.ShapeDtypeStruct((2, hidden), F32),
        ],
        compiler_params=params(),
        cost_estimate=pl.CostEstimate(
            flops=8 * pairs * slab * model * hidden, bytes_accessed=40_000_000, transcendentals=0),
        name="experts",
    )(order, own, peer, img, txt, scale, up, up_bias, down)


def expert_grads_kernel(dims, own, peer, act, dup, ddown, ce, ca, cu, cd, out, acc):
    patches, caption, ip, tp, quarter, width = dims
    slab = ip + tp
    i = pl.program_id(0)

    def add(src):
        for m, lo, hi in ((0, 0, ip), (1, ip, slab)):
            count = quarter * (hi - lo)
            e = src[:, lo:hi, :].reshape(count, -1)
            acc[m] += t_dot(e, dup[:, lo:hi, :].reshape(count, -1))

    @pl.when(i == 0)
    def _():
        for m in range(2):
            acc[m] = t_dot(ce[m], cu[m])
            acc[2 + m] = t_dot(cd[m], ca[m])

    for m, lo, hi in ((0, 0, ip), (1, ip, slab)):
        count = quarter * (hi - lo)
        acc[2 + m] += t_dot(ddown[:, lo:hi, :].reshape(count, -1), act[:, lo:hi, :].reshape(count, -1))

    @pl.when(i < 2)
    def _():
        add(own)

    @pl.when(i >= 2)
    def _():
        add(peer)

    @pl.when(i == 3)
    def _():
        out[...] = acc[...].astype(BF16)


def expert_grads(dims, own, peer, act, dup, ddown, ce, ca, cu, cd):
    patches, caption, ip, tp, quarter, width = dims
    model = own.shape[-1]
    hidden = act.shape[-1]
    slab = ip + tp
    assert hidden == model
    whole = lambda a: pl.BlockSpec(a.shape, lambda i: (0,) * a.ndim)
    first = pl.BlockSpec((quarter, slab, model), lambda i: (jnp.minimum(i, 1), 0, 0))
    last = pl.BlockSpec((quarter, slab, model), lambda i: (jnp.maximum(i - 2, 0), 0, 0))
    block = pl.BlockSpec((quarter, slab, hidden), lambda i: (i, 0, 0))
    return pl.pallas_call(
        functools.partial(expert_grads_kernel, dims),
        grid=(4,),
        in_specs=[first, last, block, block, block, whole(ce), whole(ca), whole(cu), whole(cd)],
        out_specs=pl.BlockSpec((4, model, hidden), lambda i: (0, 0, 0)),
        scratch_shapes=[pltpu.VMEM((4, model, hidden), F32)],
        out_shape=jax.ShapeDtypeStruct((4, model, hidden), BF16),
        compiler_params=params(),
        cost_estimate=pl.CostEstimate(
            flops=4 * 4 * quarter * slab * model * hidden, bytes_accessed=40_000_000, transcendentals=0),
        name="expert_grads",
    )(own, peer, act, dup, ddown, ce, ca, cu, cd)


def class_forward_kernel(e, up, up_bias, down, out):
    for m in range(2):
        u = dot(e[m], up[m]) + up_bias[m:m + 1]
        out[m] = dot(gelu_low(u), down[m])


def class_forward(e, up, up_bias, down):
    return pl.pallas_call(
        class_forward_kernel,
        out_shape=jax.ShapeDtypeStruct(e.shape, F32),
        compiler_params=params(),
        cost_estimate=pl.CostEstimate(flops=200_000_000, bytes_accessed=5_000_000, transcendentals=0),
        name="class_forward",
    )(e, up, up_bias, down)


def class_back_kernel(e, cot, dclass, scale, up, up_bias, down, act, dup, ddown, dexp, bias_grad):
    for m in range(2):
        u = dot(e[m], up[m]) + up_bias[m:m + 1]
        big, small = gelu_parts(u)
        act[m] = (u * big).astype(BF16)
        g = ((cot[m] + dclass[m]) * scale[...]).astype(BF16)
        ddown[m] = g
        du = dot_t(g, down[m]) * (big + u * small)
        bias_grad[m:m + 1, :] = jnp.sum(du, axis=0, keepdims=True)
        low = du.astype(BF16)
        dup[m] = low
        dexp[m] = dot_t(low, up[m])


def class_back(e, cot, dclass, scale, up, up_bias, down):
    hidden = up.shape[-1]
    shape = e.shape[:2] + (hidden,)
    return pl.pallas_call(
        class_back_kernel,
        out_shape=[
            jax.ShapeDtypeStruct(shape, BF16),
            jax.ShapeDtypeStruct(shape, BF16),
            jax.ShapeDtypeStruct(e.shape, BF16),
            jax.ShapeDtypeStruct(e.shape, F32),
            jax.ShapeDtypeStruct((2, hidden), F32),
        ],
        compiler_params=params(),
        cost_estimate=pl.CostEstimate(flops=300_000_000, bytes_accessed=5_000_000, transcendentals=0),
        name="class_back",
    )(e, cot, dclass, scale, up, up_bias, down)


def contrast_kernel(cls, gain, shift, weight, scale, head_in, dproj, dcls, gains, shifts, scalars):
    total = cls.shape[1]
    sharp = jnp.exp(scale[...])
    normal, inverse, proj, unit, embed = [], [], [], [], []
    for m in range(2):
        n, r = normalise(cls[m])
        h = (n * gain[m:m + 1] + shift[m:m + 1]).astype(BF16)
        head_in[m] = h
        y = dot(h, weight[m])
        u = lax.rsqrt(jnp.sum(y * y, axis=-1, keepdims=True) + 1e-6)
        normal.append(n)
        inverse.append(r)
        proj.append(y)
        unit.append(u)
        embed.append((y * u).astype(BF16))
    logits = sharp * dot_t(embed[0], embed[1])
    row_max = jnp.max(logits, axis=1, keepdims=True)
    row_lse = row_max + jnp.log(jnp.sum(jnp.exp(logits - row_max), axis=1, keepdims=True))
    col_max = jnp.max(logits, axis=0, keepdims=True)
    col_lse = col_max + jnp.log(jnp.sum(jnp.exp(logits - col_max), axis=0, keepdims=True))
    same = (lax.broadcasted_iota(jnp.int32, (total, total), 0)
            == lax.broadcasted_iota(jnp.int32, (total, total), 1))
    both = jnp.exp(logits - row_lse) + jnp.exp(logits - col_lse)
    dlogits = jnp.where(same, both - 2.0, both) * (1.0 / (2 * total))
    diagonal = jnp.sum(jnp.where(same, logits, 0.0), axis=1, keepdims=True)
    loss = (jnp.sum(row_lse - diagonal, keepdims=True) + jnp.sum(col_lse, keepdims=True)
            - jnp.sum(diagonal, keepdims=True)) * (1.0 / (2 * total))
    slope = jnp.sum(jnp.sum(dlogits * logits, axis=1, keepdims=True), axis=0, keepdims=True)
    scalars[0:1, :] = jnp.broadcast_to(loss.reshape(1, 1), (1, 128))
    scalars[1:2, :] = jnp.broadcast_to(slope, (1, 128))
    high = lax.Precision.HIGHEST
    wide = [e.astype(F32) for e in embed]
    dembed = [
        sharp * jnp.dot(dlogits, wide[1], precision=high, preferred_element_type=F32),
        sharp * lax.dot_general(dlogits, wide[0], (((0,), (0,)), ((), ())), precision=high,
                                preferred_element_type=F32),
    ]
    for m in range(2):
        u, y, d = unit[m], proj[m], dembed[m]
        dp = (u * d - u * u * u * y * jnp.sum(y * d, axis=-1, keepdims=True)).astype(BF16)
        dproj[m] = dp
        dh = dot_t(dp, weight[m])
        gains[m:m + 1, :] = jnp.sum(dh * normal[m], axis=0, keepdims=True)
        shifts[m:m + 1, :] = jnp.sum(dh, axis=0, keepdims=True)
        dcls[m] = norm_back(normal[m], inverse[m], dh * gain[m:m + 1])


def contrast(cls, gain, shift, weight, scale):
    model = cls.shape[-1]
    return pl.pallas_call(
        contrast_kernel,
        out_shape=[
            jax.ShapeDtypeStruct(cls.shape, BF16),
            jax.ShapeDtypeStruct(cls.shape[:2] + (weight.shape[-1],), BF16),
            jax.ShapeDtypeStruct(cls.shape, F32),
            jax.ShapeDtypeStruct((2, model), F32),
            jax.ShapeDtypeStruct((2, model), F32),
            jax.ShapeDtypeStruct((2, 128), F32),
        ],
        compiler_params=params(),
        cost_estimate=pl.CostEstimate(flops=1_000_000_000, bytes_accessed=5_000_000, transcendentals=0),
        name="contrast",
    )(cls, gain, shift, weight, scale)


def load_rows(dims, p, img, txt, rows):
    patches, caption, ip, tp, quarter, width = dims
    rows[0:patches, :] = img[p].astype(F32)
    rows[ip:ip + caption, :] = txt[p].astype(F32)


def final_kernel(dims, order, keep, recv, far, attended, img, txt, dclass, scale, bias, fin_img, fin_txt, sums, rows, cls):
    patches, caption, ip, tp, quarter, width = dims
    rows[...] = jnp.zeros_like(rows)
    sums[...] = jnp.zeros_like(sums)
    cls[...] = jnp.zeros_like(cls)

    def one(p, c):
        load_rows(dims, p, img, txt, rows)
        rows[0:1, :] += dclass[p, 0:1, :]
        rows[ip:ip + 1, :] += dclass[p, 1:2, :]
        d = keep[p].astype(F32) + recv[p].astype(F32) + far[p].astype(F32)
        for m, lo, hi in ((0, 0, ip), (1, ip, ip + tp)):
            b = d[lo:hi] + bias[m:m + 1]
            f = attended[p, lo:hi, :] + scale[...] * b
            if m == 0:
                fin_img[p] = f[0:patches].astype(BF16)
            else:
                fin_txt[p] = f[0:caption].astype(BF16)
            g = rows[lo:hi, :]
            sums[0:1, :] += jnp.sum(g * b, axis=0, keepdims=True)
            sums[1 + m:2 + m, :] += jnp.sum(g, axis=0, keepdims=True) * scale[...]
        return c

    lax.fori_loop(0, quarter, one, 0)


def final_rows(dims, order, keep, recv, far, attended, img, txt, dclass, scale, bias):
    patches, caption, ip, tp, quarter, width = dims
    model = img.shape[-1]
    slab = ip + tp
    whole = lambda a: pl.BlockSpec(a.shape, lambda i, o: (0,) * a.ndim)
    block = pl.BlockSpec((quarter, slab, model), lambda i, o: (0, 0, 0))
    return pl.pallas_call(
        functools.partial(final_kernel, dims),
        grid_spec=pltpu.PrefetchScalarGridSpec(
            num_scalar_prefetch=1,
            grid=(1,),
            in_specs=[
                block, block, block, block,
                pl.BlockSpec((quarter, patches, model), lambda i, o: (o[0], 0, 0)),
                pl.BlockSpec((quarter, caption, model), lambda i, o: (o[0], 0, 0)),
                whole(dclass), whole(scale), whole(bias),
            ],
            out_specs=[
                pl.BlockSpec((quarter, patches, model), lambda i, o: (0, 0, 0)),
                pl.BlockSpec((quarter, caption, model), lambda i, o: (0, 0, 0)),
                pl.BlockSpec((3, model), lambda i, o: (0, 0)),
            ],
            scratch_shapes=[pltpu.VMEM((slab, model), F32), pltpu.VMEM((8, model), F32)],
        ),
        out_shape=[
            jax.ShapeDtypeStruct((quarter, patches, model), BF16),
            jax.ShapeDtypeStruct((quarter, caption, model), BF16),
            jax.ShapeDtypeStruct((3, model), F32),
        ],
        compiler_params=params(),
        cost_estimate=pl.CostEstimate(flops=20_000_000, bytes_accessed=10_000_000, transcendentals=0),
        name="final_rows",
    )(order, keep, recv, far, attended, img, txt, dclass, scale, bias)


def norm_two_kernel(dims, order, keep, recv, far, extra, attended, a_keep, a_recv, img, txt, dclass,
                    gain, scale, bias, dattended, dattn, sums, rows, ups):
    patches, caption, ip, tp, quarter, width = dims
    rows[...] = jnp.zeros_like(rows)
    sums[...] = jnp.zeros_like(sums)

    def one(p, c):
        load_rows(dims, p, img, txt, rows)
        rows[0:1, :] += dclass[p, 0:1, :]
        rows[ip:ip + 1, :] += dclass[p, 1:2, :]
        ups[...] = keep[p].astype(F32) + recv[p].astype(F32) + far[p].astype(F32)
        ups[0:1, :] += extra[p, 0:1, :]
        ups[ip:ip + 1, :] += extra[p, 1:2, :]
        for m, lo, hi in ((0, 0, ip), (1, ip, ip + tp)):
            n, r = normalise(attended[p, lo:hi, :])
            dy = ups[lo:hi, :]
            sums[m:m + 1, :] += jnp.sum(dy * n, axis=0, keepdims=True)
            sums[2 + m:3 + m, :] += jnp.sum(dy, axis=0, keepdims=True)
            d = rows[lo:hi, :] + norm_back(n, r, dy * gain[m:m + 1])
            dattended[p, lo:hi, :] = d
            sd = d * scale[...]
            dattn[p, lo:hi, :] = sd.astype(BF16)
            a = a_keep[p, lo:hi, :].astype(F32) + a_recv[p, lo:hi, :].astype(F32) + bias[...]
            sums[4:5, :] += jnp.sum(d * a, axis=0, keepdims=True)
            sums[5:6, :] += jnp.sum(sd, axis=0, keepdims=True)
        return c

    lax.fori_loop(0, quarter, one, 0)


def norm_two(dims, order, keep, recv, far, extra, attended, a_keep, a_recv, img, txt, dclass, gain, scale, bias):
    patches, caption, ip, tp, quarter, width = dims
    model = img.shape[-1]
    slab = ip + tp
    whole = lambda a: pl.BlockSpec(a.shape, lambda i, o: (0,) * a.ndim)
    block = pl.BlockSpec((quarter, slab, model), lambda i, o: (0, 0, 0))
    return pl.pallas_call(
        functools.partial(norm_two_kernel, dims),
        grid_spec=pltpu.PrefetchScalarGridSpec(
            num_scalar_prefetch=1,
            grid=(1,),
            in_specs=[
                block, block, block, whole(extra), block, block, block,
                pl.BlockSpec((quarter, patches, model), lambda i, o: (o[0], 0, 0)),
                pl.BlockSpec((quarter, caption, model), lambda i, o: (o[0], 0, 0)),
                whole(dclass), whole(gain), whole(scale), whole(bias),
            ],
            out_specs=[block, block, pl.BlockSpec((6, model), lambda i, o: (0, 0))],
            scratch_shapes=[pltpu.VMEM((slab, model), F32), pltpu.VMEM((slab, model), F32)],
        ),
        out_shape=[
            jax.ShapeDtypeStruct((quarter, slab, model), F32),
            jax.ShapeDtypeStruct((quarter, slab, model), BF16),
            jax.ShapeDtypeStruct((6, model), F32),
        ],
        compiler_params=params(),
        cost_estimate=pl.CostEstimate(flops=40_000_000, bytes_accessed=15_000_000, transcendentals=0),
        name="norm_two",
    )(order, keep, recv, far, extra, attended, a_keep, a_recv, img, txt, dclass, gain, scale, bias)


def attend_back_kernel(dims, order, lens, d_own, d_peer, normed, qkv, mixed, wt, ow,
                       keep, send, grad_own, grad_peer, col_sums, dattn, dmixed, dqkv, acc):
    patches, caption, ip, tp, quarter, width = dims
    i = pl.program_id(0)
    slab = ip + tp
    count = quarter * slab
    model = normed.shape[-1]

    @pl.when(i == 0)
    def _():
        dattn[...] = d_own[...]
        acc[...] = jnp.zeros_like(acc)
        col_sums[...] = jnp.zeros_like(col_sums)

    @pl.when(i == 1)
    def _():
        dattn[...] = d_peer[...]

    d_rows = dattn[...].reshape(count, model)
    dmixed[...] = dot_t(d_rows, ow[...]).astype(BF16).reshape(quarter, slab, width)
    low = lax.broadcasted_iota(jnp.int32, (1, 128), 1) < HEAD_DIM
    img_ok = lax.broadcasted_iota(jnp.int32, (1, ip), 1) < patches
    txt_at = lax.broadcasted_iota(jnp.int32, (1, tp), 1)
    eighth = HEAD_DIM ** -0.5

    def one_pair(p, c):
        length = lens[order[2 * i] * quarter + p]
        for lo, hi, ok in ((0, ip, img_ok), (ip, slab, txt_at < length)):
            for g in range(width // 128):
                c0 = slice(g * 128, (g + 1) * 128)
                c1 = slice(width + g * 128, width + (g + 1) * 128)
                c2 = slice(2 * width + g * 128, 2 * width + (g + 1) * 128)
                q = qkv[p, lo:hi, c0] * jnp.asarray(eighth, BF16)
                k = qkv[p, lo:hi, c1]
                v = qkv[p, lo:hi, c2]
                do = dmixed[p, lo:hi, c0]
                dqs, dks, dvs = [], [], []
                for sel in (low, ~low):
                    s = dot_t(jnp.where(sel, q, jnp.zeros_like(q)), k)
                    w = softmax_rows(jnp.where(ok, s, NEG))
                    dw = dot_t(jnp.where(sel, do, jnp.zeros_like(do)), v)
                    dvs.append(t_dot(w.astype(BF16), do))
                    ds = (w * (dw - jnp.sum(w * dw, axis=-1, keepdims=True))).astype(BF16)
                    dqs.append(dot(ds, k))
                    dks.append(t_dot(ds, q))
                dqkv[p, lo:hi, c0] = (jnp.where(low, dqs[0], dqs[1]) * eighth).astype(BF16)
                dqkv[p, lo:hi, c1] = jnp.where(low, dks[0], dks[1]).astype(BF16)
                dqkv[p, lo:hi, c2] = jnp.where(low, dvs[0], dvs[1]).astype(BF16)
        return c

    lax.fori_loop(0, quarter, one_pair, 0)
    dp = dqkv[...].reshape(count, 3 * width)
    part = dot(dp, wt[...]).astype(BF16).reshape(quarter, slab, model)
    acc[:, 0:3 * width] += t_dot(normed[...].reshape(count, model), dp)
    acc[:, 3 * width:] += t_dot(d_rows, mixed[...].reshape(count, width))
    col_sums[...] += jnp.sum(dp.astype(F32), axis=0, keepdims=True)

    @pl.when(i == 0)
    def _():
        keep[...] = part

    @pl.when(i == 1)
    def _():
        send[...] = part
        half = width // 2
        for t in range(4):
            grad_own[:, t * half:(t + 1) * half] = acc[:, t * width:t * width + half].astype(BF16)
            grad_peer[:, t * half:(t + 1) * half] = acc[:, t * width + half:(t + 1) * width].astype(BF16)


def attend_back(dims, order, lens, d_own, d_peer, normed, qkv, mixed, wt, ow):
    patches, caption, ip, tp, quarter, width = dims
    model = normed.shape[-1]
    slab = ip + tp
    whole = lambda a: pl.BlockSpec(a.shape, lambda i, o, n: (0,) * a.ndim)
    one = pl.BlockSpec((quarter, slab, model), lambda i, o, n: (0, 0, 0))
    step = lambda cols: pl.BlockSpec((quarter, slab, cols), lambda i, o, n: (2 * i, 0, 0))
    grad = pl.BlockSpec((model, 2 * width), lambda i, o, n: (0, 0))
    return pl.pallas_call(
        functools.partial(attend_back_kernel, dims),
        grid_spec=pltpu.PrefetchScalarGridSpec(
            num_scalar_prefetch=2,
            grid=(2,),
            in_specs=[one, one, step(model), step(3 * width), step(width), whole(wt), whole(ow)],
            out_specs=[one, one, grad, grad, pl.BlockSpec((1, 3 * width), lambda i, o, n: (0, 0))],
            scratch_shapes=[
                pltpu.VMEM((quarter, slab, model), BF16),
                pltpu.VMEM((quarter, slab, width), BF16),
                pltpu.VMEM((quarter, slab, 3 * width), BF16),
                pltpu.VMEM((model, 4 * width), F32),
            ],
        ),
        out_shape=[
            jax.ShapeDtypeStruct((quarter, slab, model), BF16),
            jax.ShapeDtypeStruct((quarter, slab, model), BF16),
            jax.ShapeDtypeStruct((model, 2 * width), BF16),
            jax.ShapeDtypeStruct((model, 2 * width), BF16),
            jax.ShapeDtypeStruct((1, 3 * width), F32),
        ],
        compiler_params=params(),
        cost_estimate=pl.CostEstimate(
            flops=4 * 2 * quarter * slab * model * width * 4, bytes_accessed=20_000_000, transcendentals=0),
        name="attend_back",
    )(order, lens, d_own, d_peer, normed, qkv, mixed, wt, ow)


def norm_one_kernel(dims, order, keep, recv, dattended, img, txt, gain, d_img, d_txt, sums, rows):
    patches, caption, ip, tp, quarter, width = dims
    rows[...] = jnp.zeros_like(rows)
    sums[...] = jnp.zeros_like(sums)

    def one(p, c):
        load_rows(dims, p, img, txt, rows)
        n, r = normalise(rows[...])
        dy = keep[p].astype(F32) + recv[p].astype(F32)
        sums[0:1, :] += jnp.sum(dy * n, axis=0, keepdims=True)
        sums[1:2, :] += jnp.sum(dy, axis=0, keepdims=True)
        d = dattended[p] + norm_back(n, r, dy * gain[...])
        d_img[p] = d[0:patches].astype(BF16)
        d_txt[p] = d[ip:ip + caption].astype(BF16)
        return c

    lax.fori_loop(0, quarter, one, 0)


def norm_one(dims, order, keep, recv, dattended, img, txt, gain):
    patches, caption, ip, tp, quarter, width = dims
    model = img.shape[-1]
    slab = ip + tp
    whole = lambda a: pl.BlockSpec(a.shape, lambda i, o: (0,) * a.ndim)
    block = pl.BlockSpec((quarter, slab, model), lambda i, o: (0, 0, 0))
    return pl.pallas_call(
        functools.partial(norm_one_kernel, dims),
        grid_spec=pltpu.PrefetchScalarGridSpec(
            num_scalar_prefetch=1,
            grid=(1,),
            in_specs=[
                block, block, block,
                pl.BlockSpec((quarter, patches, model), lambda i, o: (o[0], 0, 0)),
                pl.BlockSpec((quarter, caption, model), lambda i, o: (o[0], 0, 0)),
                whole(gain),
            ],
            out_specs=[
                pl.BlockSpec((quarter, patches, model), lambda i, o: (0, 0, 0)),
                pl.BlockSpec((quarter, caption, model), lambda i, o: (0, 0, 0)),
                pl.BlockSpec((2, model), lambda i, o: (0, 0)),
            ],
            scratch_shapes=[pltpu.VMEM((slab, model), F32)],
        ),
        out_shape=[
            jax.ShapeDtypeStruct((quarter, patches, model), BF16),
            jax.ShapeDtypeStruct((quarter, caption, model), BF16),
            jax.ShapeDtypeStruct((2, model), F32),
        ],
        compiler_params=params(),
        cost_estimate=pl.CostEstimate(flops=20_000_000, bytes_accessed=10_000_000, transcendentals=0),
        name="norm_one",
    )(order, keep, recv, dattended, img, txt, gain)


def swap(value, axis, bit):
    size = lax.axis_size(axis)
    return lax.ppermute(value, axis, [(j, j ^ bit) for j in range(size)])


def to_core(value):
    return swap(value, "mp", 1)


def to_y(value):
    return swap(value, "mp", 2)


def sum_over(value, axis):
    bit = 1
    while bit < lax.axis_size(axis):
        value = value + swap(value, axis, bit)
        bit *= 2
    return value


def gather_batch(value):
    at = lax.axis_index("batch")
    bit = 1
    while bit < lax.axis_size("batch"):
        other = swap(value, "batch", bit)
        mine_first = (at & bit) == 0
        value = jnp.concatenate(
            [jnp.where(mine_first, value, other), jnp.where(mine_first, other, value)], axis=1)
        bit *= 2
    return value


def absolute(value, quarter, me):
    parts = [value[:, r * quarter:(r + 1) * quarter] for r in range(4)]
    by_xor = [parts[ORDER.index(x)] for x in range(4)]
    out = []
    for q in range(4):
        pick = by_xor[q]
        for m in range(1, 4):
            pick = jnp.where(me == m, by_xor[q ^ m], pick)
        out.append(pick)
    return jnp.concatenate(out, axis=1)


def gather_rows(own, me):
    quarter = own.shape[0]
    near = jnp.stack([own, to_y(own)])
    far = to_core(near)
    out = jnp.zeros((4,) + own.shape, own.dtype)
    for r, value in enumerate((near[0], near[1], far[0], far[1])):
        out = lax.dynamic_update_slice(out, value[None], (me ^ ORDER[r],) + (0,) * own.ndim)
    return out.reshape((4 * quarter,) + own.shape[1:])


def add_low(a, b):
    return (a.astype(F32) + b.astype(F32)).astype(BF16)


def per_device(
    image_states, text_states, caption_lengths, image_cotangent, text_cotangent,
    first_gain, first_shift, query_key_value, query_value_bias, output_weight, output_bias,
    attention_scale, expert_gain, expert_shift, expert_up, expert_up_bias, expert_down,
    expert_down_bias, feedforward_scale, head_gain, head_shift, head_weight, logit_scale,
):
    pairs, patches, model = image_states.shape
    caption = text_states.shape[1]
    local = query_key_value.shape[2]
    width = 2 * local
    quarter = pairs // 4
    assert lax.axis_size("mp") == 4 and pairs == 4 * quarter and width % 128 == 0
    ip, tp = up16(patches), up16(caption)
    dims = (patches, caption, ip, tp, quarter, width)
    me = lax.axis_index("mp")
    batch_at = lax.axis_index("batch")
    batch_size = lax.axis_size("batch")
    order = me ^ jnp.asarray(ORDER, jnp.int32)
    row = lambda v: v.reshape(1, -1)

    own_w = jnp.transpose(query_key_value, (1, 2, 0)).reshape(3 * local, model)
    both = jnp.concatenate([own_w, output_weight])
    far = to_y(both)
    far_bias = to_y(query_value_bias)
    wt = jnp.concatenate(
        [own_w.reshape(3, local, model), far[:3 * local].reshape(3, local, model)], axis=1
    ).reshape(3 * width, model)
    ow = jnp.concatenate([output_weight, far[3 * local:]])
    bias_pair = jnp.concatenate([query_value_bias, far_bias], axis=1)
    bias = jnp.concatenate([bias_pair[0], jnp.zeros_like(bias_pair[0]), bias_pair[1]]).reshape(1, -1)

    normed, qkv, mixed, a_keep, a_send = attend(
        dims, order, caption_lengths, image_states, text_states, row(first_gain), row(first_shift), wt, bias, ow)
    a_recv = to_core(a_send)
    attended, e_own = residual(
        dims, order, a_keep, a_recv, image_states, text_states, row(attention_scale), row(output_bias),
        expert_gain, expert_shift)
    e_peer = to_core(e_own)

    pad = lambda v: jnp.pad(v, ((0, 0), (0, up16(pairs) - pairs), (0, 0)))
    class_of = lambda v: jnp.stack([v[:, 0], v[:, ip]])
    class_att = class_of(attended)
    class_att = jnp.concatenate([class_att, to_core(class_att)], axis=1)
    class_e = pad(jnp.concatenate([class_of(e_own), class_of(e_peer)], axis=1))
    class_cot = jnp.stack([image_cotangent[:, 0], text_cotangent[:, 0]]).astype(F32)
    class_cot = class_cot.reshape(2, 4, quarter, model)
    class_cot = jnp.concatenate(
        [lax.dynamic_index_in_dim(class_cot, order[r], 1, keepdims=False) for r in range(4)], axis=1)

    def sum_mp(value):
        other = to_core(value)
        value = value + jnp.concatenate([other[:, 2 * quarter:], other[:, :2 * quarter]], axis=1)
        other = to_y(value)
        parts = [other[:, r * quarter:(r + 1) * quarter] for r in (1, 0, 3, 2)]
        return value + jnp.concatenate(parts, axis=1)

    class_down = sum_mp(class_forward(class_e, expert_up, expert_up_bias, expert_down)[:, :pairs])
    class_final = class_att + feedforward_scale * (class_down + expert_down_bias[:, None, :])
    all_class = gather_batch(absolute(class_final, quarter, me))
    head_in, dproj, dcls, grad_head_gain, grad_head_shift, scalars = contrast(
        all_class, head_gain, head_shift, head_weight, logit_scale.reshape(1, 1))
    contrast_loss = scalars[0, :1]
    grad_logit_scale = scalars[1, :1]
    cols = model // batch_size
    head_cols = lax.dynamic_slice_in_dim(head_in, batch_at * cols, cols, axis=2)
    grad_head_weight = jnp.einsum("mnc,mne->mce", head_cols, dproj, preferred_element_type=F32)
    mine = lax.dynamic_slice_in_dim(dcls, batch_at * pairs, pairs, axis=1).reshape(2, 4, quarter, model)
    dclass = jnp.concatenate(
        [lax.dynamic_index_in_dim(mine, order[r], 1, keepdims=False) for r in range(4)], axis=1)
    c_act, c_dup, c_ddown, c_dexp, c_bias = class_back(
        class_e, pad(class_cot), pad(dclass), row(feedforward_scale), expert_up, expert_up_bias, expert_down)
    extra = sum_mp(c_dexp[:, :pairs])[:, :quarter]
    extra = jnp.transpose(extra, (1, 0, 2))
    dclass_own = jnp.transpose(dclass[:, :quarter], (1, 0, 2))

    act, dup, ddown, d_keep, d_send, x_keep, x_send, up_bias_part = experts(
        dims, order, e_own, e_peer, image_cotangent, text_cotangent, row(feedforward_scale),
        expert_up, expert_up_bias, expert_down)
    x_recv = to_core(x_send)
    x_far = to_y(add_low(x_keep[quarter:], x_recv[quarter:]))
    d_recv = to_core(d_send)
    d_far = to_y(add_low(d_keep[quarter:], d_recv[quarter:]))
    expert_grad = expert_grads(dims, e_own, e_peer, act, dup, ddown, class_e, c_act, c_dup, c_ddown)
    expert_grad = lax.psum_scatter(expert_grad, "batch", scatter_dimension=1, tiled=True).astype(F32)
    grad_expert_up = expert_grad[:2]
    grad_expert_down = jnp.transpose(expert_grad[2:], (0, 2, 1))

    dattended, dattn, sums_two = norm_two(
        dims, order, x_keep, x_recv, x_far, extra, attended, a_keep, a_recv, image_cotangent, text_cotangent,
        dclass_own, expert_gain, row(attention_scale), row(output_bias))
    dattn_peer = to_core(dattn)
    fin_img, fin_txt, sums_fin = final_rows(
        dims, order, d_keep, d_recv, d_far, attended, image_cotangent, text_cotangent, dclass_own,
        row(feedforward_scale), expert_down_bias)
    image_output = gather_rows(fin_img, me)
    text_output = gather_rows(fin_txt, me)

    n_keep, n_send, grad_own, grad_peer, col_sums = attend_back(
        dims, order, caption_lengths, dattn, dattn_peer, normed, qkv, mixed, wt, ow)
    n_recv = to_core(n_send)
    d_img, d_txt, sums_one = norm_one(
        dims, order, n_keep, n_recv, dattended, image_states, text_states, row(first_gain))
    image_grad = gather_rows(d_img, me)
    text_grad = gather_rows(d_txt, me)

    attn_grad = jnp.concatenate([grad_own, grad_peer], axis=1)
    attn_grad = lax.psum_scatter(attn_grad, "batch", scatter_dimension=0, tiled=True)
    attn_grad = attn_grad[:, :2 * width].astype(F32) + to_y(attn_grad[:, 2 * width:]).astype(F32)
    grad_query_key_value = attn_grad[:, :3 * local].reshape(cols, 3, local)
    grad_output_weight = jnp.transpose(attn_grad[:, 3 * local:])

    own_sums = jnp.concatenate([sums_one, sums_two, sums_fin])
    own_sums = sum_over(own_sums, "mp")
    heads = col_sums.reshape(3, 2, local)[::2]
    heads = heads[:, 0] + to_y(heads[:, 1])
    up_sums = up_bias_part + c_bias
    flat = jnp.concatenate([own_sums.reshape(-1), heads.reshape(-1), up_sums.reshape(-1)])
    count = flat.shape[0]
    flat = jnp.pad(flat, (0, -count % 1024)).reshape(-1, 128)
    flat = sum_over(flat, "batch").reshape(-1)[:count]
    rows_done = own_sums.shape[0]
    own_sums = flat[:rows_done * model].reshape(rows_done, model)
    heads = flat[rows_done * model:rows_done * model + 2 * local].reshape(2, local)
    grad_expert_up_bias = flat[rows_done * model + 2 * local:].reshape(up_sums.shape)
    mine = lax.dynamic_slice_in_dim(own_sums, batch_at * cols, cols, axis=1)
    head_gain_mine = lax.dynamic_slice_in_dim(grad_head_gain, batch_at * cols, cols, axis=1)
    head_shift_mine = lax.dynamic_slice_in_dim(grad_head_shift, batch_at * cols, cols, axis=1)
    return (
        image_output,
        text_output,
        contrast_loss,
        image_grad,
        text_grad,
        mine[0],
        mine[1],
        grad_query_key_value,
        heads,
        grad_output_weight,
        mine[7],
        mine[6],
        mine[2:4],
        mine[4:6],
        grad_expert_up,
        grad_expert_up_bias,
        grad_expert_down,
        mine[9:11],
        mine[8],
        head_gain_mine,
        head_shift_mine,
        grad_head_weight,
        grad_logit_scale,
    )


def solution(mesh):
    return jax.shard_map(
        per_device,
        mesh=mesh,
        in_specs=(
            P("batch", None, None),
            P("batch", None, None),
            P("batch"),
            P("batch", None, None),
            P("batch", None, None),
            P(),
            P(),
            P(None, None, "mp"),
            P(None, "mp"),
            P("mp", None),
            P(),
            P(),
            P(),
            P(),
            P(None, None, "mp"),
            P(None, "mp"),
            P(None, "mp", None),
            P(),
            P(),
            P(),
            P(),
            P(),
            P(),
        ),
        out_specs=(
            P("batch", None, None),
            P("batch", None, None),
            P(),
            P("batch", None, None),
            P("batch", None, None),
            P("batch"),
            P("batch"),
            P("batch", None, "mp"),
            P(None, "mp"),
            P("mp", "batch"),
            P("batch"),
            P("batch"),
            P(None, "batch"),
            P(None, "batch"),
            P(None, "batch", "mp"),
            P(None, "mp"),
            P(None, "mp", "batch"),
            P(None, "batch"),
            P("batch"),
            P(None, "batch"),
            P(None, "batch"),
            P(None, "batch", None),
            P(),
        ),
        check_vma=False,
    )
```

time: 1690 us -> 466 us (0.28)
  waiting for transfers between devices: 1030 us -> 143 us
  blocking collectives: 185 us -> 0 us
  Pallas kernels: 0 us -> 181 us
  matrix products: 146 us -> 2.19 us
  other arithmetic: 129 us -> 21.4 us
  local copies, waits for them, and re-layouts: 166 us -> 61.3 us
  starting transfers between devices: 0.96 us -> 24.4 us
    psum x4 -> x0, waiting for transfers between devices: 474 us -> none  [the longest x1 161 us: per_device(): attention_out = lax.psum(attention_part, 'mp')]
    unnamed x21 -> x2, waiting for transfers between devices: 286 us -> 0.03 us
    reduce_scatter x3 -> x2, waiting for transfers between devices: 269 us -> 15.3 us  [the longest x1 15.3 us: per_device(): lax.psum_scatter(expert_grad, 'batch', scatter_dimension=1, tiled=True)]
    pallas_call x0 -> x11, Pallas kernels: none -> 181 us  [the longest x1 50 us: attend_back(): pl.pallas_call(functools.partial(attend_back_kernel, dims), grid_spec=plt...]
    dot_general x41 -> x1, matrix products: 143 us -> 2.19 us  [per_device(): jnp.einsum('mnc,mne->mce', head_cols, dproj, preferred_element_type=F32)]
    ppermute x0 -> x33, waiting for transfers between devices: none -> 128 us  [swap(): return lax.ppermute(value, axis, [(j, j ^ bit) for j in range(size)])]
    all_gather x4 -> x0, blocking collectives: 123 us -> none  [the longest x1 31 us: per_device(): text_piece = lax.all_gather(text_float, 'batch', axis=0, tiled=True)]
    reduce_sum x21 -> x0, other arithmetic: 69.7 us -> none  [the longest x6 22.4 us: layer_norm(): centred = values - jnp.mean(values, axis=-1, keepdims=True)]
  transfers between devices with their start and end apart: 14 -> 35, of which waited for: 11 -> 19; matrix products, arithmetic and copies ran while one was open for 15% -> 14% of each run, Pallas kernels for 0% -> 16%
where the time goes in v1:
time: 466 us; the launch traced here: 457 us
  Pallas kernels  181 us (39%)
  waiting for transfers between devices  143 us (31%)
  local copies, waits for them, and re-layouts  61.3 us (13%)
  starting transfers between devices  24.4 us (5%)
  between operations  23.7 us (5%)
  other arithmetic  21.4 us (5%)
    ppermute x33, waiting for transfers between devices, swap(): return lax.ppermute(value, axis, [(j, j ^ bit) for j in range(size)])  128 us
    pallas_call x1, Pallas kernels, attend_back(): pl.pallas_call(functools.partial(attend_back_kernel, dims), grid_spec=plt...  50 us
    pallas_call x1, Pallas kernels, attend(): pl.pallas_call(functools.partial(attend_kernel, dims), grid_spec=pltpu.Pr...  38.9 us
    pallas_call x1, Pallas kernels, experts(): pl.pallas_call(functools.partial(expert_kernel, dims), grid_spec=pltpu.Pr...  29.7 us
    ppermute x33, starting transfers between devices, swap(): return lax.ppermute(value, axis, [(j, j ^ bit) for j in range(size)])  24.3 us
    pallas_call x1, Pallas kernels, expert_grads(): pl.pallas_call(functools.partial(expert_grads_kernel, dims), grid=(4,), i...  18.7 us
    reduce_scatter x1, waiting for transfers between devices, per_device(): lax.psum_scatter(expert_grad, 'batch', scatter_dimension=1, tiled=True)  15.3 us
    dynamic_update_slice x16, local copies, waits for them, and re-layouts, gather_rows(): lax.dynamic_update_slice(out, value[None], (me ^ ORDER[r],) + (0,) * own....  10.8 us
  transfers between devices with their start and end apart: 35, of which 19 were waited for; matrix products, arithmetic and copies ran while one was open for 14% of the time, Pallas kernels for 16%

profile of v1, /device:TPU:0, one launch (start us, length us, event | category | flops | bytes accessed | tf_op | source)
XLA Modules:
  0.0 457.2 jit_solution(12516906137233895934)
XLA Ops:
  8.7 3.0 collective-permute-start
  14.1 23.6 %collective-permute-done.1 = f32[2,192]{1,0:T(2,128)S(1)} collective-permute-done((f32[2,192]{1,0:T(2,128)S(1)}, f32[2,192]{1,0:T(2,128)S(1)}, u32[]{:S(2)}, u32[]{:S(2)}) %collective-permute-start.1) | collective-permute-done | bytes 1568 | tf_op jit(solution)/shard_map/ppermute | solution.py:775
  40.7 38.9 %attend.1 = (bf16[12,256,768]{2,1,0:T(8,128)(2,1)}, bf16[12,256,1152]{2,1,0:T(8,128)(2,1)}, bf16[12,256,384]{2,1,0:T(8,128)(2,1)}, bf16[6,256,768]{2,1,0:T(8,128)(2,1)}, bf16[6,256,768]{2,1,0:T(8,128)(2,1)}) custom-call(s32[4]{0:T(128)} %broadcast_xor_fusion.order, s32[12]{0:T(128)} %lens.3, bf16[12,197,768]{2,1,0:T(8,128)(2,1)} %img.11, ...), custom_call_target="tpu_custom_call" | custom-call | flops 7247757312 | bytes 30000000 | tf_op jit(solution)/shard_map/attend/pallas_call | solution.py:129
  80.8 3.5 collective-permute-done.2.recv.a_recv
  85.7 7.3 %residual.1 = (f32[6,256,768]{2,1,0:T(8,128)}, bf16[6,256,768]{2,1,0:T(8,128)(2,1)}) custom-call(s32[4]{0:T(128)} %broadcast_xor_fusion.order, bf16[6,256,768]{2,1,0:T(8,128)(2,1)} %get-tuple-element.63.keep.a_keep, bf16[6,256,768]{2,1,0:T(8,128)(2,1)} %copy-done.1, bf16[12,197,768]{2,1,0:T(8,128)(2,1)} %img.11, bf16[12,40,768]{2,1,0:T(8,128)(2,1)} %txt.11, ...), custom_call_target="tpu_custom_call" | custom-call | flops 40000000 | bytes 20000000 | tf_op jit(solution)/shard_map/residual/pallas_call | solution.py:189
  93.9 3.2 copy.79
  97.0 2.8 copy.77
  101.5 4.0 class_forward.1
  109.8 29.7 %experts.1 = (bf16[12,256,768]{2,1,0:T(8,128)(2,1)}, bf16[12,256,768]{2,1,0:T(8,128)(2,1)}, bf16[12,256,768]{2,1,0:T(8,128)(2,1)}, bf16[6,256,768]{2,1,0:T(8,128...) custom-call(s32[4]{0:T(128)} %broadcast_xor_fusion.order, ...), custom_call_target="tpu_custom_call" | custom-call | flops 14495514624 | bytes 40000000 | tf_op jit(solution)/shard_map/experts/pallas_call | solution.py:280
  142.4 2.7 collective-permute-done.9
  157.0 2.7 collective-permute-start.11
  160.4 12.1 %collective-permute-done.11 = f32[2,48,768]{2,1,0:T(8,128)S(1)} collective-permute-done((f32[2,48,768]{2,1,0:T(8,128)S(1)}, f32[2,48,768]{2,1,0:T(8,128)S(1)}, u32[]{:S(2)}, u32[]{:S(2)}) %collective-permute-start.11) | collective-permute-done | bytes 294944 | tf_op jit(solution)/shard_map/ppermute | solution.py:775
  173.4 5.5 %contrast.1 = (bf16[2,96,768]{2,1,0:T(8,128)(2,1)}, bf16[2,96,768]{2,1,0:T(8,128)(2,1)}, f32[2,96,768]{2,1,0:T(8,128)}, f32[2,768]{1,0:T(2,128)}, f32[2,768]{1,0:T(2,128)}, /*index=5*/f32[2,128]{1,0:T(2,128)}) custom-call(f32[2,96,768]{2,1,0:T(8,128)} %pad_maximum_fusion.6.cls, f32[2,768]{1,0:T(2,128)} %gain.4, f32[2,768]{1,0:T(2,128)} %shift.3, ...), custom_call_target="tpu_custom_call" | custom-call | flops 1000000000 | bytes 5000000 | tf_op jit(solution)/shard_map/contrast/pallas_call | solution.py:469
  183.2 5.0 %class_back.1 = (bf16[2,16,768]{2,1,0:T(8,128)(2,1)}, bf16[2,16,768]{2,1,0:T(8,128)(2,1)}, bf16[2,16,768]{2,1,0:T(8,128)(2,1)}, f32[2,16,768]{2,1,0:T(8,128)}, f32[2,768]{1,0:T(2,128)}) custom-call(bf16[2,16,768]{2,1,0:T(8,128)(2,1)} %fusion.7.e.ce, f32[2,16,768]{2,1,0:T(8,128)} %select_maximum_fusion.cot, f32[2,16,768]{2,1,0:T(8,128)} %pad.17.clone.dclass, ...), custom_call_target="tpu_custom_call" | custom-call | flops 300000000 | bytes 5000000 | tf_op jit(solution)/shard_map/class_back/pallas_call | solution.py:405
  192.3 19.3 %collective-permute-done.19 = f32[2,12,768]{2,0,1:T(2,128)S(1)} collective-permute-done((f32[2,12,768]{2,0,1:T(2,128)S(1)}, f32[2,12,768]{2,0,1:T(2,128)S(1)}, u32[]{:S(2)}, u32[]{:S(2)}) %collective-permute-start.19) | collective-permute-done | bytes 73760 | tf_op jit(solution)/shard_map/ppermute | solution.py:775
  213.3 9.1 %norm_two.1 = (f32[3,256,768]{2,1,0:T(8,128)}, bf16[3,256,768]{2,1,0:T(8,128)(2,1)}, f32[6,768]{1,0:T(8,128)}) custom-call(s32[4]{0:T(128)} %broadcast_xor_fusion.order, bf16[6,256,768]{2,1,0:T(8,128)(2,1)} %get-tuple-element.73.keep, bf16[6,256,768]{2,1,0:T(8,128)(2,1)} %collective-permute-done.16.recv, bf16[3,256,768]{2,1,0:T(8,128)(2,1)} %copy-done.9, ...), custom_call_target="tpu_custom_call" | custom-call | flops 40000000 | bytes 15000000 | tf_op jit(solution)/shard_map/norm_two/pallas_call | solution.py:588
  222.4 3.1 collective-permute-done.20.d_peer
  226.5 50.0 %attend_back.1 = (bf16[3,256,768]{2,1,0:T(8,128)(2,1)}, bf16[3,256,768]{2,1,0:T(8,128)(2,1)}, bf16[768,768]{1,0:T(8,128)(2,1)}, bf16[768,768]{1,0:T(8,128)(2,1)}, f32[1,1152]{1,0:T(1,128)}) custom-call(s32[4]{0:T(128)} %broadcast_xor_fusion.order, s32[12]{0:T(128)} %lens.3, bf16[3,256,768]{2,1,0:T(8,128)(2,1)} %get-tuple-element.76.d_own, ...), custom_call_target="tpu_custom_call" | custom-call | flops 7247757312 | bytes 20000000 | tf_op jit(solution)/shard_map/attend_back/pallas_call | solution.py:691
  276.5 3.2 pad_maximum_fusion
  280.0 18.7 %expert_grads.1 = bf16[4,768,768]{2,1,0:T(8,128)(2,1)} custom-call(bf16[6,256,768]{2,1,0:T(8,128)(2,1)} %get-tuple-element.65.own, bf16[6,256,768]{2,1,0:T(8,128)(2,1)} %collective-permute-done.3.peer, bf16[12,256,768]{2,1,0:T(8,128)(2,1)} %get-tuple-element.93.act, bf16[12,256,768]{2,1,0:T(8,128)(2,1)} %get-tuple-element.94.dup, ...), custom_call_target="tpu_custom_call" | custom-call | flops 7247757312 | bytes 40000000 | tf_op jit(solution)/shard_map/expert_grads/pallas_call | solution.py:358
  308.5 21.7 %collective-permute-done.5.far = bf16[3,256,768]{2,1,0:T(8,128)(2,1)S(1)} collective-permute-done((bf16[3,256,768]{2,1,0:T(8,128)(2,1)S(1)}, bf16[3,256,768]{2,1,0:T(8,128)(2,1)S(1)}, u32[]{:S(2)}, u32[]{:S(2)}) %collective-permute-start.5) | collective-permute-done | bytes 1179680 | tf_op jit(solution)/shard_map/ppermute | solution.py:775
  331.2 6.4 %final_rows.1 = (bf16[3,197,768]{2,1,0:T(8,128)(2,1)}, bf16[3,40,768]{2,1,0:T(8,128)(2,1)}, f32[3,768]{1,0:T(4,128)}) custom-call(s32[4]{0:T(128)} %broadcast_xor_fusion.order, bf16[6,256,768]{2,1,0:T(8,128)(2,1)} %get-tuple-element.66.keep, bf16[6,256,768]{2,1,0:T(8,128)(2,1)} %collective-permute-done.4.recv, bf16[3,256,768]{2,1,0:T(8,128)(2,1)} %copy-done.12, ...), custom_call_target="tpu_custom_call" | custom-call | flops 20000000 | bytes 10000000 | tf_op jit(solution)/shard_map/final_rows/pallas_call | solution.py:523
  340.0 5.4 %collective-permute-done.14 = bf16[3,40,768]{2,1,0:T(8,128)(2,1)S(1)} collective-permute-done((bf16[3,40,768]{2,1,0:T(8,128)(2,1)}, bf16[3,40,768]{2,1,0:T(8,128)(2,1)S(1)}, u32[]{:S(2)}, u32[]{:S(2)}) %collective-permute-start.14) | collective-permute-done | bytes 184352 | tf_op jit(solution)/shard_map/ppermute | solution.py:775
  347.2 16.5 %collective-permute-done.12 = bf16[3,197,768]{2,1,0:T(8,128)(2,1)S(1)} collective-permute-done((bf16[3,197,768]{2,1,0:T(8,128)(2,1)}, bf16[3,197,768]{2,1,0:T(8,128)(2,1)S(1)}, u32[]{:S(2)}, u32[]{:S(2)}) %collective-permute-start.12) | collective-permute-done | bytes 907808 | tf_op jit(solution)/shard_map/ppermute | solution.py:775
  364.0 2.6 copy.84
  369.7 6.4 %norm_one.1 = (bf16[3,197,768]{2,1,0:T(8,128)(2,1)}, bf16[3,40,768]{2,1,0:T(8,128)(2,1)}, f32[2,768]{1,0:T(2,128)}) custom-call(s32[4]{0:T(128)} %broadcast_xor_fusion.order, bf16[3,256,768]{2,1,0:T(8,128)(2,1)} %get-tuple-element.80.keep, bf16[3,256,768]{2,1,0:T(8,128)(2,1)} %copy-done.11, f32[3,256,768]{2,1,0:T(8,128)} %get-tuple-element.82.dattended, ...), custom_call_target="tpu_custom_call" | custom-call | flops 20000000 | bytes 10000000 | tf_op jit(solution)/shard_map/norm_one/pallas_call | solution.py:744
  388.0 7.1 %collective-permute-done.30 = f32[88,128]{1,0:T(8,128)S(1)} collective-permute-done((f32[88,128]{1,0:T(8,128)S(1)}, f32[88,128]{1,0:T(8,128)S(1)}, u32[]{:S(2)}, u32[]{:S(2)}) %collective-permute-start.30) | collective-permute-done | bytes 45088 | tf_op jit(solution)/shard_map/ppermute | solution.py:775
  397.9 2.8 collective-permute-done.31
  409.9 2.5 fusion.22
  418.9 2.5 fusion.21
  425.7 4.1 collective-permute-done.32
  431.7 15.3 %reduce-scatter.5.cloned.1.call-done = bf16[4,96,768]{2,1,0:T(8,128)(2,1)} async-done(((bf16[4,768,768]{2,1,0:T(8,128)(2,1)}), bf16[4,96,768]{2,1,0:T(8,128)(2,1)}) %reduce-scatter.5.cloned.1.call-update) | async-done | bytes 589840 | tf_op jit(solution)/shard_map/reduce_scatter | solution.py:915
  (240 shorter events, 92.9 us)
Async XLA Ops:
  7.2 415.2 %reduce-scatter.3.cloned.1.call-start = ((), (), s32[]{:S(2)}) async-start(), calls=%async_computation.2 | async-start | bytes 2654208 | tf_op jit(solution)/shard_map/reduce_scatter | solution.py:938
  8.7 29.8 %collective-permute-start = (bf16[768,768]{1,0:T(8,128)(2,1)S(1)}, bf16[768,768]{1,0:T(8,128)(2,1)S(1)}, u32[]{:S(2)}, u32[]{:S(2)}) collective-permute-start(bf16[768,768]{1,0:T(8,128)(2,1)S(1)} %pad_maximum_fusion.4), channel_id=1, source_target_pairs={{0,2},{1,3},{2,0},{3,1},{4,6},{5,7},{6,4},{7,5},{8,10},{9,11},{10,... | collective-permute-start | bytes 3538952 | tf_op jit(solution)/shard_map/ppermute | solution.py:775
  11.7 26.0 %collective-permute-start.1 = (f32[2,192]{1,0:T(2,128)S(1)}, f32[2,192]{1,0:T(2,128)S(1)}, u32[]{:S(2)}, u32[]{:S(2)}) collective-permute-start(f32[2,192]{1,0:T(2,128)S(1)} %copy-done.30), channel_id=1, source_target_pairs={{0,2},{1,3},{2,0},{3,1},{4,6},{5,7},{6,4},{7,5},{8,10},{9,11},{10,... | collective-permute-start | bytes 4616 | tf_op jit(solution)/shard_map/ppermute | solution.py:775
  79.6 4.7 %collective-permute-start.2 = (bf16[6,256,768]{2,1,0:T(8,128)(2,1)}, bf16[6,256,768]{2,1,0:T(8,128)(2,1)S(1)}, u32[]{:S(2)}, u32[]{:S(2)}) collective-permute-start(bf16[6,256,768]{2,1,0:T(8,128)(2,1)} %get-tuple-element.64), channel_id=1, source_target_pairs={{0,1},{1,0},{2,3},{3,2},{4,5},{5,4},{6,7},{7,6},{8,9},{9,8},{10,11... | collective-permute-start | bytes 7077896 | tf_op jit(solution)/shard_map/ppermute | solution.py:775
  93.1 6.8 %collective-permute-start.3 = (bf16[6,256,768]{2,1,0:T(8,128)(2,1)}, bf16[6,256,768]{2,1,0:T(8,128)(2,1)}, u32[]{:S(2)}, u32[]{:S(2)}) collective-permute-start(bf16[6,256,768]{2,1,0:T(8,128)(2,1)} %get-tuple-element.65.own), channel_id=1, source_target_pairs={{0,1},{1,0},{2,3},{3,2},{4,5},{5,4},{6,7},{7,6},{8,9},{9,8},{10,11... | collective-permute-start | bytes 7077896 | tf_op jit(solution)/shard_map/ppermute | solution.py:775
  105.8 33.9 %collective-permute-start.6 = (f32[2,6,768]{2,1,0:T(8,128)S(1)}, f32[2,6,768]{2,1,0:T(8,128)S(1)}, u32[]{:S(2)}, u32[]{:S(2)}) collective-permute-start(f32[2,6,768]{2,1,0:T(8,128)S(1)} %pad_maximum_fusion.13), channel_id=1, source_target_pairs={{0,1},{1,0},{2,3},{3,2},{4,5},{5,4},{6,7},{7,6},{8,9},{9,8},{10,11... | collective-permute-start | bytes 110600 | tf_op jit(solution)/shard_map/ppermute | solution.py:775
  108.0 31.7 %collective-permute-start.8 = (f32[2,12,768]{2,1,0:T(8,128)S(1)}, f32[2,12,768]{2,1,0:T(8,128)S(1)}, u32[]{:S(2)}, u32[]{:S(2)}) collective-permute-start(f32[2,12,768]{2,1,0:T(8,128)S(1)} %maximum_add_fusion.1), channel_id=1, source_target_pairs={{0,2},{1,3},{2,0},{3,1},{4,6},{5,7},{6,4},{7,5},{8,10},{9,11},{10,... | collective-permute-start | bytes 221192 | tf_op jit(solution)/shard_map/ppermute | solution.py:775
  139.5 40.9 %collective-permute-start.16 = (bf16[6,256,768]{2,1,0:T(8,128)(2,1)}, bf16[6,256,768]{2,1,0:T(8,128)(2,1)}, u32[]{:S(2)}, u32[]{:S(2)}) collective-permute-start(bf16[6,256,768]{2,1,0:T(8,128)(2,1)} %get-tuple-element.74), channel_id=1, source_target_pairs={{0,1},{1,0},{2,3},{3,2},{4,5},{5,4},{6,7},{7,6},{8,9},{9,8},{10,11... | collective-permute-start | bytes 7077896 | tf_op jit(solution)/shard_map/ppermute | solution.py:775
  139.8 5.2 %collective-permute-start.9 = (f32[2,12,768]{2,1,0:T(8,128)S(1)}, f32[2,12,768]{2,1,0:T(8,128)S(1)}, u32[]{:S(2)}, u32[]{:S(2)}) collective-permute-start(f32[2,12,768]{2,1,0:T(8,128)S(1)} %pad_maximum_fusion.11), channel_id=1, source_target_pairs={{0,4},{4,0},{8,12},{12,8},{16,20},{20,16},{24,28},{28,24},{1,5},{5... | collective-permute-start | bytes 221192 | tf_op jit(solution)/shard_map/ppermute | solution.py:775
  145.2 11.7 %collective-permute-start.10 = (f32[2,24,768]{2,1,0:T(8,128)S(1)}, f32[2,24,768]{2,1,0:T(8,128)S(1)}, u32[]{:S(2)}, u32[]{:S(2)}) collective-permute-start(f32[2,24,768]{2,1,0:T(8,128)S(1)} %pad_maximum_fusion.10), channel_id=1, source_target_pairs={{0,8},{4,12},{8,0},{12,4},{16,24},{20,28},{24,16},{28,20},{1,9},{5... | collective-permute-start | bytes 442376 | tf_op jit(solution)/shard_map/ppermute | solution.py:775
  157.0 15.5 %collective-permute-start.11 = (f32[2,48,768]{2,1,0:T(8,128)S(1)}, f32[2,48,768]{2,1,0:T(8,128)S(1)}, u32[]{:S(2)}, u32[]{:S(2)}) collective-permute-start(f32[2,48,768]{2,1,0:T(8,128)S(1)} %pad_maximum_fusion.9), channel_id=1, source_target_pairs={{0,16},{4,20},{8,24},{12,28},{16,0},{20,4},{24,8},{28,12},{1,17},{... | collective-permute-start | bytes 884744 | tf_op jit(solution)/shard_map/ppermute | solution.py:775
  182.0 30.2 %collective-permute-start.17 = (bf16[3,256,768]{2,1,0:T(8,128)(2,1)S(1)}, bf16[3,256,768]{2,1,0:T(8,128)(2,1)S(1)}, u32[]{:S(2)}, u32[]{:S(2)}) collective-permute-start(bf16[3,256,768]{2,1,0:T(8,128)(2,1)S(1)} %add_convert_fusion), channel_id=1, source_target_pairs={{0,2},{1,3},{2,0},{3,1},{4,6},{5,7},{6,4},{7,5},{8,10},{9,11},{10,... | collective-permute-start | bytes 3538952 | tf_op jit(solution)/shard_map/ppermute | solution.py:775
  190.5 21.0 %collective-permute-start.19 = (f32[2,12,768]{2,0,1:T(2,128)S(1)}, f32[2,12,768]{2,0,1:T(2,128)S(1)}, u32[]{:S(2)}, u32[]{:S(2)}) collective-permute-start(f32[2,12,768]{2,0,1:T(2,128)S(1)} %maximum_add_fusion.3), channel_id=1, source_target_pairs={{0,2},{1,3},{2,0},{3,1},{4,6},{5,7},{6,4},{7,5},{8,10},{9,11},{10,... | collective-permute-start | bytes 221192 | tf_op jit(solution)/shard_map/ppermute | solution.py:775
  222.4 3.1 collective-permute-start.20
  279.7 167.3 %reduce-scatter.5.cloned.1.call-start = ((), (), s32[]{:S(2)}) async-start(), calls=%async_computation.3 | async-start | bytes 5308416 | tf_op jit(solution)/shard_map/reduce_scatter | solution.py:915
  279.8 18.9 %collective-permute-start.4 = (bf16[6,256,768]{2,1,0:T(8,128)(2,1)}, bf16[6,256,768]{2,1,0:T(8,128)(2,1)}, u32[]{:S(2)}, u32[]{:S(2)}) collective-permute-start(bf16[6,256,768]{2,1,0:T(8,128)(2,1)} %get-tuple-element.67), channel_id=1, source_target_pairs={{0,1},{1,0},{2,3},{3,2},{4,5},{5,4},{6,7},{7,6},{8,9},{9,8},{10,11... | collective-permute-start | bytes 7077896 | tf_op jit(solution)/shard_map/ppermute | solution.py:775
  302.0 28.2 %collective-permute-start.5 = (bf16[3,256,768]{2,1,0:T(8,128)(2,1)S(1)}, bf16[3,256,768]{2,1,0:T(8,128)(2,1)S(1)}, u32[]{:S(2)}, u32[]{:S(2)}) collective-permute-start(bf16[3,256,768]{2,1,0:T(8,128)(2,1)S(1)} %add_convert_fusion.1), channel_id=1, source_target_pairs={{0,2},{1,3},{2,0},{3,1},{4,6},{5,7},{6,4},{7,5},{8,10},{9,11},{10,... | collective-permute-start | bytes 3538952 | tf_op jit(solution)/shard_map/ppermute | solution.py:775
  337.6 7.8 %collective-permute-start.14 = (bf16[3,40,768]{2,1,0:T(8,128)(2,1)}, bf16[3,40,768]{2,1,0:T(8,128)(2,1)S(1)}, u32[]{:S(2)}, u32[]{:S(2)}) collective-permute-start(bf16[3,40,768]{2,1,0:T(8,128)(2,1)} %get-tuple-element.71), channel_id=1, source_target_pairs={{0,2},{1,3},{2,0},{3,1},{4,6},{5,7},{6,4},{7,5},{8,10},{9,11},{10,... | collective-permute-start | bytes 552968 | tf_op jit(solution)/shard_map/ppermute | solution.py:775
  338.2 25.6 %collective-permute-start.12 = (bf16[3,197,768]{2,1,0:T(8,128)(2,1)}, bf16[3,197,768]{2,1,0:T(8,128)(2,1)S(1)}, u32[]{:S(2)}, u32[]{:S(2)}) collective-permute-start(bf16[3,197,768]{2,1,0:T(8,128)(2,1)} %get-tuple-element.70), channel_id=1, source_target_pairs={{0,2},{1,3},{2,0},{3,1},{4,6},{5,7},{6,4},{7,5},{8,10},{9,11},{10,... | collective-permute-start | bytes 2723336 | tf_op jit(solution)/shard_map/ppermute | solution.py:775
  345.4 1.8 collective-permute-start.15
  345.5 23.1 %collective-permute-start.21 = (bf16[3,256,768]{2,1,0:T(8,128)(2,1)}, bf16[3,256,768]{2,1,0:T(8,128)(2,1)S(1)}, u32[]{:S(2)}, u32[]{:S(2)}) collective-permute-start(bf16[3,256,768]{2,1,0:T(8,128)(2,1)} %get-tuple-element.81), channel_id=1, source_target_pairs={{0,1},{1,0},{2,3},{3,2},{4,5},{5,4},{6,7},{7,6},{8,9},{9,8},{10,11... | collective-permute-start | bytes 3538952 | tf_op jit(solution)/shard_map/ppermute | solution.py:775
  366.6 43.3 %collective-permute-start.13 = (bf16[2,3,197,768]{3,0,2,1:T(2,128)(2,1)}, bf16[2,3,197,768]{3,0,2,1:T(2,128)(2,1)S(1)}, u32[]{:S(2)}, u32[]{:S(2)}) collective-permute-start(bf16[2,3,197,768]{3,0,2,1:T(2,128)(2,1)} %copy.84), channel_id=1, source_target_pairs={{0,1},{1,0},{2,3},{3,2},{4,5},{5,4},{6,7},{7,6},{8,9},{9,8},{10,11... | collective-permute-start | bytes 5446664 | tf_op jit(solution)/shard_map/ppermute | solution.py:775
  377.4 3.6 collective-permute-start.28
  379.0 4.2 collective-permute-start.27
  381.1 14.1 %collective-permute-start.24 = (bf16[3,40,768]{2,1,0:T(8,128)(2,1)}, bf16[3,40,768]{2,1,0:T(8,128)(2,1)}, u32[]{:S(2)}, u32[]{:S(2)}) collective-permute-start(bf16[3,40,768]{2,1,0:T(8,128)(2,1)} %get-tuple-element.84), channel_id=1, source_target_pairs={{0,2},{1,3},{2,0},{3,1},{4,6},{5,7},{6,4},{7,5},{8,10},{9,11},{10,... | collective-permute-start | bytes 552968 | tf_op jit(solution)/shard_map/ppermute | solution.py:775
  381.6 25.5 %collective-permute-start.22 = (bf16[3,197,768]{2,1,0:T(8,128)(2,1)}, bf16[3,197,768]{2,1,0:T(8,128)(2,1)}, u32[]{:S(2)}, u32[]{:S(2)}) collective-permute-start(bf16[3,197,768]{2,1,0:T(8,128)(2,1)} %get-tuple-element.83), channel_id=1, source_target_pairs={{0,2},{1,3},{2,0},{3,1},{4,6},{5,7},{6,4},{7,5},{8,10},{9,11},{10,... | collective-permute-start | bytes 2723336 | tf_op jit(solution)/shard_map/ppermute | solution.py:775
  383.2 4.6 %collective-permute-start.29 = (f32[88,128]{1,0:T(8,128)S(1)}, f32[88,128]{1,0:T(8,128)S(1)}, u32[]{:S(2)}, u32[]{:S(2)}) collective-permute-start(f32[88,128]{1,0:T(8,128)S(1)} %fusion.11), channel_id=1, source_target_pairs={{0,4},{4,0},{8,12},{12,8},{16,20},{20,16},{24,28},{28,24},{1,5},{5... | collective-permute-start | bytes 135176 | tf_op jit(solution)/shard_map/ppermute | solution.py:775
  387.8 7.3 %collective-permute-start.30 = (f32[88,128]{1,0:T(8,128)S(1)}, f32[88,128]{1,0:T(8,128)S(1)}, u32[]{:S(2)}, u32[]{:S(2)}) collective-permute-start(f32[88,128]{1,0:T(8,128)S(1)} %fusion.32), channel_id=1, source_target_pairs={{0,8},{4,12},{8,0},{12,4},{16,24},{20,28},{24,16},{28,20},{1,9},{5... | collective-permute-start | bytes 135176 | tf_op jit(solution)/shard_map/ppermute | solution.py:775
  395.1 5.6 %collective-permute-start.31 = (f32[88,128]{1,0:T(8,128)S(1)}, f32[88,128]{1,0:T(8,128)S(1)}, u32[]{:S(2)}, u32[]{:S(2)}) collective-permute-start(f32[88,128]{1,0:T(8,128)S(1)} %fusion.33), channel_id=1, source_target_pairs={{0,16},{4,20},{8,24},{12,28},{16,0},{20,4},{24,8},{28,12},{1,17},{... | collective-permute-start | bytes 135176 | tf_op jit(solution)/shard_map/ppermute | solution.py:775
  396.9 17.6 %collective-permute-start.25 = (bf16[2,3,40,768]{3,2,1,0:T(8,128)(2,1)}, bf16[2,3,40,768]{3,2,1,0:T(8,128)(2,1)}, u32[]{:S(2)}, u32[]{:S(2)}) collective-permute-start(bf16[2,3,40,768]{3,2,1,0:T(8,128)(2,1)} %pad_maximum_fusion.8), channel_id=1, source_target_pairs={{0,1},{1,0},{2,3},{3,2},{4,5},{5,4},{6,7},{7,6},{8,9},{9,8},{10,11... | collective-permute-start | bytes 1105928 | tf_op jit(solution)/shard_map/ppermute | solution.py:775
  409.8 9.1 %collective-permute-start.23 = (bf16[2,3,197,768]{3,0,2,1:T(2,128)(2,1)S(1)}, bf16[2,3,197,768]{3,0,2,1:T(2,128)(2,1)S(1)}, u32[]{:S(2)}, u32[]{:S(2)}) collective-permute-start(bf16[2,3,197,768]{3,0,2,1:T(2,128)(2,1)S(1)} %copy.89), channel_id=1, source_target_pairs={{0,1},{1,0},{2,3},{3,2},{4,5},{5,4},{6,7},{7,6},{8,9},{9,8},{10,11... | collective-permute-start | bytes 5446664 | tf_op jit(solution)/shard_map/ppermute | solution.py:775
  423.5 6.3 %collective-permute-start.32 = (bf16[96,768]{1,0:T(8,128)(2,1)S(1)}, bf16[96,768]{1,0:T(8,128)(2,1)S(1)}, u32[]{:S(2)}, u32[]{:S(2)}) collective-permute-start(bf16[96,768]{1,0:T(8,128)(2,1)S(1)} %slice.331), channel_id=1, source_target_pairs={{0,2},{1,3},{2,0},{3,1},{4,6},{5,7},{6,4},{7,5},{8,10},{9,11},{10,... | collective-permute-start | bytes 442376 | tf_op jit(solution)/shard_map/ppermute | solution.py:775
  (35 other events, 339.5 us)
Sparse Core Ops, SparseCore 0:
  279.8 67.1 reduce-scatter.2
  350.6 96.2 reduce-scatter.4
